TPU v7x, 256 devices: a whole 4x4x8 slice. The times are simulated.
256 devices in a mesh: row: 32 (over x_hi, z, core), col: 8 (over x_lo, y).
Axes of the slice: x: 4 (x_hi: 2, x_lo: 2; x = x_hi * 2 + x_lo), y: 4, z: 8, core: 2. Of those that a mesh axis runs over, the one named last changes fastest.
Arguments:
- pair: bfloat16 [64, 2048, 2048], P(None, 'row', 'col'), may hold values from -6 to 6
- conv_weight: bfloat16 [9, 64, 64], replicated, may hold values from -0.25 to 0.25
- conv_bias: float32 [64], replicated, may hold values from -3 to 3
- single: bfloat16 [2048, 384], P('col'), may hold values from -6 to 6
- quat_vec: float32 [3, 2048], P(None, 'col'), may hold values from -6 to 6
- trans: float32 [3, 2048], P(None, 'col'), may hold values from -200 to 200
- chain_id: int32 [2048], P('col'), may hold values from 0 to 7, never falling along the last dimension, each value on 1 to 512 neighbouring positions
- residue_mask: int32 [2048], P('col'), may hold values 0 or 1
- w_query: bfloat16 [384, 192], replicated, may hold values from -0.3125 to 0.3125
- w_key: bfloat16 [384, 192], replicated, may hold values from -0.3125 to 0.3125
- w_value: bfloat16 [384, 192], replicated, may hold values from -0.3125 to 0.3125
- w_qpts: bfloat16 [384, 144], replicated, may hold values from -0.3125 to 0.3125
- w_kvpts: bfloat16 [384, 432], replicated, may hold values from -0.3125 to 0.3125
- w_bias: bfloat16 [12, 64], replicated, may hold values from -0.75 to 0.75
- head_weight: float32 [12], replicated, may hold values from -1.5 to 1
- chain_weight: float32 [12], replicated, may hold values from -2 to 2
- w_out: bfloat16 [1248, 384], replicated, may hold values from -0.15625 to 0.15625
- ln_gain: float32 [384], replicated, may hold values from 0.5 to 1.5
Outputs:
- pair_out: bfloat16 [64, 2048, 2048], P(None, 'row', 'col')
- single_out: bfloat16 [2048, 384], P('row')
All inputs are finite; a program needn't handle non-finite values. No bound on the sum of `residue_mask` on one device may be relied on, other than what follows from the above.
Results may differ from a plain program's by a relative error of at most 0.0034.
Values may be sent and summed in bfloat16 or wider, within the bound.
No kernel may reach another device: no remote copies, remote signals or barrier semaphores. Data moves between devices by JAX's collectives and lax.ppermute only.
A program may use at most 128 MiB of HBM per device.

v0:
```python
import math

import jax
import jax.numpy as jnp
import numpy as np
from jax import lax
from jax.experimental import pallas as pl
from jax.experimental.pallas import tpu as pltpu
from jax.sharding import PartitionSpec as P

DILATION_STEP = 8


logit_scale = math.sqrt(1.0 / 3.0)
mask_penalty = 10000.0
norm_eps = 1e-05
highest = lax.Precision.HIGHEST


def edge_cells(rows):
    head = jnp.concatenate([row[:, :DILATION_STEP] for row in rows], axis=1)
    tail = jnp.concatenate([row[:, row.shape[1] - DILATION_STEP :] for row in rows], axis=1)
    return head, tail


def turn_kernel(pair_ref, rows_ref, head_ref, tail_ref):
    turned = jnp.swapaxes(pair_ref[...], 0, 1)
    rows_ref[...] = turned
    for block in range(turned.shape[0] // 8):
        head, tail = edge_cells([turned[8 * block + i] for i in range(8)])
        head_ref[block] = head
        tail_ref[block] = tail


def turn(pair):
    channels, row_count, col_count = pair.shape
    step = 16
    edge = jax.ShapeDtypeStruct((row_count // 8, channels, 64), pair.dtype)
    return pl.pallas_call(
        turn_kernel,
        grid=(row_count // step,),
        in_specs=[pl.BlockSpec((channels, step, col_count), lambda b: (0, b, 0))],
        out_specs=[
            pl.BlockSpec((step, channels, col_count), lambda b: (b, 0, 0)),
            pl.BlockSpec((step // 8, channels, 64), lambda b: (b, 0, 0)),
            pl.BlockSpec((step // 8, channels, 64), lambda b: (b, 0, 0)),
        ],
        out_shape=[
            jax.ShapeDtypeStruct((row_count, channels, col_count), pair.dtype),
            edge,
            edge,
        ],
        name="turn",
    )(pair)


def rim_kernel(up_ref, down_ref, head_ref, tail_ref):
    for index, ref in enumerate((up_ref, down_ref)):
        head, tail = edge_cells([ref[i] for i in range(8)])
        head_ref[index] = head
        tail_ref[index] = tail


def rim(up, down):
    edge = jax.ShapeDtypeStruct((2, up.shape[1], 64), up.dtype)
    return pl.pallas_call(rim_kernel, out_shape=[edge, edge], name="rim")(up, down)


def main_kernel(
    up_ref,
    own_ref,
    down_ref,
    left_ref,
    right_ref,
    weight_ref,
    bias_ref,
    head_bias_ref,
    base_ref,
    value_ref,
    owner_ref,
    out_ref,
    sums_ref,
    window_ref,
    soft_ref,
):
    step = pl.program_id(0)
    last = pl.num_programs(0) - 1
    channels = own_ref.shape[1]
    cols = own_ref.shape[2]
    slot = lax.rem(step, 3)

    def stage(source):
        for i in range(8):
            cells = source[i]
            cut = slice(8 * i, 8 * i + 8)
            window_ref[slot, i, 0:channels] = jnp.concatenate(
                [left_ref[0][:, cut], cells[:, : cols - 8]], axis=1
            )
            window_ref[slot, i, channels : 2 * channels] = cells
            window_ref[slot, i, 2 * channels : 3 * channels] = jnp.concatenate(
                [cells[:, 8:], right_ref[0][:, cut]], axis=1
            )

    @pl.when(step == 0)
    def _():
        stage(up_ref)

    @pl.when(jnp.logical_and(step > 0, step < last))
    def _():
        stage(own_ref)

    @pl.when(step == last)
    def _():
        stage(down_ref)

    @pl.when(step >= 2)
    def _():
        first = lax.rem(step + 1, 3)
        middle = lax.rem(step + 2, 3)
        lane = lax.broadcasted_iota(jnp.int32, (16, 128), 1)
        for i in range(8):
            conv = (
                jnp.dot(weight_ref[0], window_ref[first, i], preferred_element_type=jnp.float32)
                + jnp.dot(weight_ref[1], window_ref[middle, i], preferred_element_type=jnp.float32)
                + jnp.dot(weight_ref[2], window_ref[slot, i], preferred_element_type=jnp.float32)
            )
            conv = conv + bias_ref[...]
            bent = jnp.where(conv > 0.0, conv, jnp.exp(jnp.minimum(conv, 0.0)) - 1.0)
            cells = window_ref[middle, i, channels : 2 * channels].astype(jnp.float32)
            updated = (cells + bent).astype(jnp.bfloat16)
            out_ref[i] = updated
            bias = jnp.dot(head_bias_ref[...], updated, preferred_element_type=jnp.float32)
            logits = base_ref[i] + logit_scale * bias
            peak = jnp.max(logits, axis=1, keepdims=True)
            weights = jnp.exp(logits - peak).astype(jnp.bfloat16)
            total = jnp.sum(weights.astype(jnp.float32), axis=1, keepdims=True)
            pair_sum = lax.dot_general(
                weights, updated, (((1,), (1,)), ((), ())), preferred_element_type=jnp.float32
            )
            padded = jnp.concatenate([pair_sum, jnp.zeros((16, 64), jnp.float32)], axis=1)
            padded = jnp.where(lane == 104, peak, jnp.where(lane == 105, total, padded))
            row = (step - 2) * 8 + i
            sums_ref[row] = padded
            soft_ref[pl.ds(pl.multiple_of(row * 16, 16), 16), :] = weights

    @pl.when(step == last)
    def _():
        chunk = 256
        sub = lax.broadcasted_iota(jnp.int32, (chunk // 16, 16, 128), 1)
        for part in range(soft_ref.shape[0] // chunk):
            soft = soft_ref[part * chunk : (part + 1) * chunk, :]
            acc = jnp.dot(soft, value_ref[0], preferred_element_type=jnp.float32) + jnp.dot(
                soft, value_ref[1], preferred_element_type=jnp.float32
            )
            acc = acc.reshape(chunk // 16, 16, 512) * owner_ref[...][None]
            folded = jnp.sum(acc, axis=1, keepdims=True)
            rows = slice(part * chunk // 16, (part + 1) * chunk // 16)
            kept = sums_ref[rows]
            for k in range(4):
                lanes = folded[:, :, 128 * k : 128 * k + 128]
                kept = jnp.where(sub == 12 + k, lanes, kept)
            sums_ref[rows] = kept


def main(up, own, down, left, right, weight, bias, head_bias, base, value, owner):
    row_count, channels, col_count = own.shape
    steps = row_count // 8 + 2
    fixed3 = lambda b: (0, 0, 0)
    fixed2 = lambda b: (0, 0)
    late = lambda b: (jnp.maximum(b - 2, 0), 0, 0)
    return pl.pallas_call(
        main_kernel,
        grid=(steps,),
        in_specs=[
            pl.BlockSpec(up.shape, fixed3),
            pl.BlockSpec((8, channels, col_count), lambda b: (jnp.clip(b - 1, 0, steps - 3), 0, 0)),
            pl.BlockSpec(down.shape, fixed3),
            pl.BlockSpec((1, channels, 64), lambda b: (b, 0, 0)),
            pl.BlockSpec((1, channels, 64), lambda b: (b, 0, 0)),
            pl.BlockSpec(weight.shape, fixed3),
            pl.BlockSpec(bias.shape, fixed2),
            pl.BlockSpec(head_bias.shape, fixed2),
            pl.BlockSpec((8, 16, col_count), late),
            pl.BlockSpec(value.shape, fixed3),
            pl.BlockSpec(owner.shape, fixed2),
        ],
        out_specs=[
            pl.BlockSpec((8, channels, col_count), late),
            pl.BlockSpec((row_count, 16, 128), fixed3),
        ],
        out_shape=[
            jax.ShapeDtypeStruct((row_count, channels, col_count), jnp.bfloat16),
            jax.ShapeDtypeStruct((row_count, 16, 128), jnp.float32),
        ],
        scratch_shapes=[
            pltpu.VMEM((3, 8, 3 * channels, col_count), jnp.bfloat16),
            pltpu.VMEM((row_count * 16, col_count), jnp.bfloat16),
        ],
        name="main",
    )(up, own, down, left, right, weight, bias, head_bias, base, value, owner)


def in_pieces(value, count):
    parts = []
    for _ in range(count - 1):
        part = value.astype(jnp.bfloat16)
        parts.append(part)
        value = value - part.astype(jnp.float32)
    parts.append(value.astype(jnp.bfloat16))
    return parts


def dot32(a, b):
    return jnp.dot(a, b, preferred_element_type=jnp.float32)


def dot32_nt(a, b):
    return lax.dot_general(a, b, (((1,), (1,)), ((), ())), preferred_element_type=jnp.float32)


def to_global(local, frame):
    span = local.shape[1] // 3
    turned = []
    for x in range(3):
        total = frame[:, 9 + x : 10 + x]
        for d in range(3):
            column = frame[:, 3 * x + d : 3 * x + d + 1]
            total = total + column * local[:, span * d : span * (d + 1)]
        turned.append(total)
    return jnp.concatenate(turned, axis=1)


def keys_kernel(
    single_ref,
    w_key_ref,
    w_value_ref,
    w_kvpts_ref,
    frame_ref,
    pick_key_ref,
    pick_value_ref,
    shift_value_ref,
    points_ref,
    value_ref,
    key_ref,
    key_sq_ref,
):
    rows = single_ref[...]
    key = dot32(rows, w_key_ref[...])
    value = dot32(rows, w_value_ref[...]).astype(jnp.bfloat16)
    points = to_global(dot32(rows, w_kvpts_ref[...]), frame_ref[...])
    point_parts = in_pieces(points, 3)
    key_parts = in_pieces(
        jnp.concatenate([key, jnp.zeros((key.shape[0], 256 - key.shape[1]), jnp.float32)], axis=1), 3
    )
    whole = jnp.zeros((rows.shape[0], 256), jnp.float32)
    for index in range(3):
        picked = dot32(point_parts[index], pick_key_ref[...])
        whole = whole + picked
        key_ref[index, :, 0:256] = key_parts[index]
        key_ref[index, :, 256:512] = picked.astype(jnp.bfloat16)
    square = jnp.zeros((16, rows.shape[0]), jnp.float32)
    for part in in_pieces(whole * whole, 3):
        square = square + dot32_nt(points_ref[...], part)
    key_sq_ref[...] = square
    value_ref[0] = (
        dot32(value, shift_value_ref[...]) + dot32(point_parts[0], pick_value_ref[...])
    ).astype(jnp.bfloat16)
    value_ref[1] = dot32(point_parts[1], pick_value_ref[...]).astype(jnp.bfloat16)


def keys(single, w_key, w_value, w_kvpts, frame, pick_key, pick_value, shift_value, points):
    count = single.shape[0]
    return pl.pallas_call(
        keys_kernel,
        out_shape=[
            jax.ShapeDtypeStruct((2, count, 512), jnp.bfloat16),
            jax.ShapeDtypeStruct((3, count, 512), jnp.bfloat16),
            jax.ShapeDtypeStruct((16, count), jnp.float32),
        ],
        name="keys",
    )(single, w_key, w_value, w_kvpts, frame, pick_key, pick_value, shift_value, points)


def base_kernel(
    query_ref,
    w_query_ref,
    w_qpts_ref,
    frame_ref,
    key_ref,
    key_sq_ref,
    factor_ref,
    column_ref,
    key_row_ref,
    base_ref,
):
    rows = query_ref[...]
    count = rows.shape[0]
    query = dot32(rows, w_query_ref[...])
    points = to_global(dot32(rows, w_qpts_ref[...]), frame_ref[...])
    points = jnp.concatenate([points, jnp.zeros((count, 256 - points.shape[1]), jnp.float32)], axis=1)
    query = jnp.concatenate([query, jnp.zeros((count, 256 - query.shape[1]), jnp.float32)], axis=1)
    factor = factor_ref[...]
    query = query[:, None, :] * factor[None, :, 0:256]
    scaled = points[:, None, :] * factor[None, :, 256:512]
    own_sq = 0.5 * jnp.sum(scaled * points[:, None, :], axis=2, keepdims=True)
    query_parts = in_pieces(query.reshape(count * 16, 256), 3)
    point_parts = in_pieces(scaled.reshape(count * 16, 256), 3)
    total = jnp.zeros((count * 16, key_ref.shape[1]), jnp.float32)
    for a, b in ((2, 0), (1, 1), (0, 2), (1, 0), (0, 1), (0, 0)):
        total = total + dot32_nt(
            jnp.concatenate([query_parts[a], point_parts[a]], axis=1), key_ref[b]
        )
    scale = column_ref[:, 0:1]
    chain = column_ref[:, 1:2]
    same = (frame_ref[:, 12:13] == key_row_ref[0:1, :]).astype(jnp.float32)
    shared = scale * key_sq_ref[...]
    base_ref[...] = (
        total.reshape(count, 16, -1)
        - own_sq
        - shared[None]
        + chain[None] * same[:, None, :]
        - key_row_ref[1:2, :][None]
    )


def base_logits(query, w_query, w_qpts, frame, key, key_sq, factor, column, key_row):
    count = query.shape[0]
    step = 16
    whole2 = lambda b: (0, 0)
    whole3 = lambda b: (0, 0, 0)
    part = lambda b: (b, 0)
    return pl.pallas_call(
        base_kernel,
        grid=(count // step,),
        in_specs=[
            pl.BlockSpec((step, query.shape[1]), part),
            pl.BlockSpec(w_query.shape, whole2),
            pl.BlockSpec(w_qpts.shape, whole2),
            pl.BlockSpec((step, frame.shape[1]), part),
            pl.BlockSpec(key.shape, whole3),
            pl.BlockSpec(key_sq.shape, whole2),
            pl.BlockSpec(factor.shape, whole2),
            pl.BlockSpec(column.shape, whole2),
            pl.BlockSpec(key_row.shape, whole2),
        ],
        out_specs=pl.BlockSpec((step, 16, key.shape[1]), whole3_at),
        out_shape=jax.ShapeDtypeStruct((count, 16, key.shape[1]), jnp.float32),
        name="base",
    )(query, w_query, w_qpts, frame, key, key_sq, factor, column, key_row)


def whole3_at(b):
    return (b, 0, 0)


def finish_kernel(
    sums_ref, owner_ref, frame_ref, single_ref, w_pair_ref, w_flat_ref, gain_ref, out_ref
):
    sums = sums_ref[...]
    parts, count = sums.shape[0], sums.shape[1]
    width = single_ref.shape[1]
    live = lax.broadcasted_iota(jnp.int32, sums.shape[:3] + (1,), 2) < 12
    peaks = jnp.where(live, sums[:, :, :, 104:105], 0.0)
    scales = jnp.exp(peaks - jnp.max(peaks, axis=0, keepdims=True))
    counts = jnp.where(live, sums[:, :, :, 105:106], 1.0)
    totals = jnp.sum(counts * scales, axis=0, keepdims=True)
    scales = scales / totals
    means = jnp.sum(sums * scales, axis=0)
    flats = []
    for k in range(4):
        own = owner_ref[:, 128 * k : 128 * k + 128]
        lanes = jnp.sum(scales * own[None, None], axis=2)
        flats.append(jnp.sum(sums[:, :, 12 + k, :] * lanes, axis=0))
    flat = jnp.concatenate(flats, axis=1)
    frame = frame_ref[...]
    centred = [flat[:, 192 + 96 * x : 288 + 96 * x] - frame[:, 9 + x : 10 + x] for x in range(3)]
    local = [
        sum(frame[:, 3 * x + d : 3 * x + d + 1] * centred[x] for x in range(3)) for d in range(3)
    ]
    flat = jnp.concatenate([flat[:, :192]] + local, axis=1)
    paired = jnp.concatenate([means[:, h, 0:64] for h in range(12)], axis=1)
    update = jnp.zeros((count, width), jnp.float32)
    for values, weights in ((paired, w_pair_ref), (flat, w_flat_ref)):
        for part in reversed(in_pieces(values, 3)):
            update = update + dot32(part, weights[...])
    hidden = single_ref[...].astype(jnp.float32) + update
    row_mean = jnp.mean(hidden, axis=1, keepdims=True)
    row_var = jnp.mean((hidden - row_mean) ** 2, axis=1, keepdims=True)
    rows = ((hidden - row_mean) * lax.rsqrt(row_var + norm_eps) * gain_ref[...]).astype(jnp.bfloat16)
    for index in range(parts):
        out_ref[index] = rows


def finish(sums, owner, frame, single, w_pair, w_flat, gain):
    parts, count = sums.shape[:2]
    return pl.pallas_call(
        finish_kernel,
        out_shape=jax.ShapeDtypeStruct((parts, count, single.shape[1]), jnp.bfloat16),
        name="finish",
    )(sums, owner, frame, single, w_pair, w_flat, gain)


def frame_columns(quat_vec, trans, chain):
    rows = jnp.concatenate([rotations(quat_vec).reshape(9, -1), trans, chain], axis=0)
    return jnp.pad(rows, ((0, 16 - rows.shape[0]), (0, 0))).T


def tables(head_count, head_dim, query_points, value_points):
    both = query_points + value_points
    span = 3 * head_count * both
    pick_key = np.zeros((span, 256), np.float32)
    pick_value = np.zeros((span, 512), np.float32)
    shift_value = np.zeros((head_count * head_dim, 512), np.float32)
    points = np.zeros((16, 256), np.float32)
    scalars = np.zeros((16, 256), np.float32)
    owner = np.zeros((16, 512), np.float32)
    for h in range(head_count):
        for d in range(head_dim):
            lane = h * head_dim + d
            scalars[h, lane] = 1.0
            owner[h, lane] = 1.0
            shift_value[lane, lane] = 1.0
        for x in range(3):
            first = (x * head_count + h) * both
            for p in range(query_points):
                lane = (x * head_count + h) * query_points + p
                pick_key[first + p, lane] = 1.0
                points[h, lane] = 1.0
            for p in range(value_points):
                lane = head_count * head_dim + (x * head_count + h) * value_points + p
                pick_value[first + query_points + p, lane] = 1.0
                owner[h, lane] = 1.0
    return pick_key, pick_value, shift_value, points, scalars, owner


def shifted(cells, axis, forward):
    count = lax.axis_size(axis)
    if forward:
        routes = [(i, i + 1) for i in range(count - 1)]
    else:
        routes = [(i + 1, i) for i in range(count - 1)]
    return lax.ppermute(cells, axis, routes)


def ring(a, b, size):
    return min((a - b) % size, (b - a) % size)


def place(row, col, n_row, n_col):
    z_count = max(n_row // 4, 1)
    y_count = max(n_col // 2, 1)
    return (row // (2 * z_count) * 2 + col // y_count, col % y_count, row // 2 % z_count)


def query_routes(n_row, n_col):
    group = n_row // n_col
    z_count = max(n_row // 4, 1)
    y_count = max(n_col // 2, 1)
    pairs, offsets = [], np.zeros((n_row, n_col), np.int32)
    for holder_col in range(n_col):
        targets = [(holder_col * group + a, c) for a in range(group) for c in range(n_col)]
        sources = list(range(n_row))
        cost = np.zeros((n_row, n_row))
        for a, (row, col) in enumerate(targets):
            there = place(row, col, n_row, n_col)
            for b in sources:
                here = place(b, holder_col, n_row, n_col)
                hops = (
                    ring(there[0], here[0], 4)
                    + ring(there[1], here[1], y_count)
                    + ring(there[2], here[2], z_count)
                )
                cost[a, b] = float(hops) ** 4
        chosen = list(range(n_row))
        changed = True
        while changed:
            changed = False
            for a in range(n_row):
                for b in range(a):
                    now = cost[a, chosen[a]] + cost[b, chosen[b]]
                    then = cost[a, chosen[b]] + cost[b, chosen[a]]
                    if then < now - 1e-9:
                        chosen[a], chosen[b] = chosen[b], chosen[a]
                        changed = True
        for a, (row, col) in enumerate(targets):
            pairs.append((chosen[a] * n_col + holder_col, row * n_col + col))
            offsets[chosen[a], holder_col] = row % group
    return pairs, offsets


def pieces(value, count):
    parts = []
    for _ in range(count - 1):
        part = lax.reduce_precision(value, 8, 7)
        parts.append(part.astype(jnp.bfloat16))
        value = value - part
    parts.append(value.astype(jnp.bfloat16))
    return parts


def rotations(quat_vec):
    comp_b = quat_vec[0]
    comp_c = quat_vec[1]
    comp_d = quat_vec[2]
    inverse_norm = 1.0 / (1.0 + comp_b * comp_b + comp_c * comp_c + comp_d * comp_d)
    first_row = jnp.stack(
        [
            1.0 + comp_b * comp_b - comp_c * comp_c - comp_d * comp_d,
            2.0 * (comp_b * comp_c - comp_d),
            2.0 * (comp_b * comp_d + comp_c),
        ]
    )
    second_row = jnp.stack(
        [
            2.0 * (comp_b * comp_c + comp_d),
            1.0 - comp_b * comp_b + comp_c * comp_c - comp_d * comp_d,
            2.0 * (comp_c * comp_d - comp_b),
        ]
    )
    third_row = jnp.stack(
        [
            2.0 * (comp_b * comp_d - comp_c),
            2.0 * (comp_c * comp_d + comp_b),
            1.0 - comp_b * comp_b - comp_c * comp_c + comp_d * comp_d,
        ]
    )
    return jnp.stack([first_row, second_row, third_row]) * inverse_norm


def per_device(
    pair,
    conv_weight,
    conv_bias,
    single,
    quat_vec,
    trans,
    chain_id,
    residue_mask,
    w_query,
    w_key,
    w_value,
    w_qpts,
    w_kvpts,
    w_bias,
    head_weight,
    chain_weight,
    w_out,
    ln_gain,
):
    channels, row_count, col_count = pair.shape
    head_count = w_bias.shape[0]
    head_dim = w_query.shape[1] // head_count
    width = single.shape[1]
    query_points = w_qpts.shape[1] // (3 * head_count)
    value_points = w_kvpts.shape[1] // (3 * head_count) - query_points
    n_row, n_col = lax.axis_size("row"), lax.axis_size("col")
    part_count = row_count // n_col

    routes, offsets = query_routes(n_row, n_col)
    packed = jnp.concatenate([quat_vec, trans, chain_id.astype(jnp.float32)[None, :]], axis=0)
    offset = jnp.asarray(offsets)[lax.axis_index("row"), lax.axis_index("col")] * row_count
    mine_single = lax.dynamic_slice_in_dim(single, offset, row_count, 0)
    mine_frames = lax.dynamic_slice_in_dim(packed, offset, row_count, 1)
    frame_rows = jnp.concatenate(pieces(mine_frames, 3), axis=0)
    message = jnp.concatenate(
        [mine_single, jnp.pad(frame_rows, ((0, 3), (0, width - row_count)))], axis=0
    )
    message = lax.ppermute(message, ("row", "col"), routes)
    query_single = message[:row_count]
    frame_rows = message[row_count : row_count + 21, :row_count].astype(jnp.float32)
    query_frames = frame_rows[0:7] + frame_rows[7:14] + frame_rows[14:21]

    own, own_head, own_tail = turn(pair)
    up = shifted(own[row_count - DILATION_STEP :], "row", True)
    down = shifted(own[:DILATION_STEP], "row", False)
    rim_head, rim_tail = rim(up, down)
    left = shifted(
        jnp.concatenate([rim_tail[:1], own_tail, rim_tail[1:]], axis=0), "col", True
    )
    right = shifted(
        jnp.concatenate([rim_head[:1], own_head, rim_head[1:]], axis=0), "col", False
    )
    pick_key, pick_value, shift_value, points, scalars, owner = tables(
        head_count, head_dim, query_points, value_points
    )
    chain = chain_id.astype(jnp.float32)[None, :]
    present = residue_mask.astype(jnp.float32)
    value, key, key_sq = keys(
        single,
        w_key,
        w_value,
        w_kvpts,
        frame_columns(quat_vec, trans, chain),
        jnp.asarray(pick_key, jnp.bfloat16),
        jnp.asarray(pick_value, jnp.bfloat16),
        jnp.asarray(shift_value, jnp.bfloat16),
        jnp.asarray(points, jnp.bfloat16),
    )
    query_frame = frame_columns(query_frames[0:3], query_frames[3:6], query_frames[6:7])
    point_scale = logit_scale * jax.nn.softplus(head_weight) * math.sqrt(2.0 / (9.0 * query_points))
    head_pad = (0, 16 - head_count)
    column = jnp.stack(
        [jnp.pad(0.5 * point_scale, head_pad), jnp.pad(chain_weight, head_pad)], axis=1
    )
    factor = jnp.concatenate(
        [
            jnp.asarray(scalars * (logit_scale / math.sqrt(head_dim)), jnp.float32),
            jnp.asarray(points, jnp.float32) * jnp.pad(point_scale, head_pad)[:, None],
        ],
        axis=1,
    )
    key_row = jnp.concatenate([chain, mask_penalty * (1.0 - present)[None, :]], axis=0)
    base = base_logits(
        query_single,
        w_query,
        w_qpts,
        query_frame,
        key,
        key_sq,
        factor,
        column,
        key_row,
    )
    owner = jnp.asarray(owner, jnp.float32)
    weight = (
        conv_weight.reshape(3, 3, channels, channels)
        .transpose(0, 2, 1, 3)
        .reshape(3, channels, 3 * channels)
    )
    updated, sums = main(
        up,
        own,
        down,
        left,
        right,
        weight,
        conv_bias[:, None],
        jnp.pad(w_bias, ((0, 16 - head_count), (0, 0))),
        base,
        value,
        owner,
    )
    pair_out = updated.transpose(1, 0, 2)
    sums = sums.reshape(n_col, part_count, 16, 128)
    sums = lax.all_to_all(sums, "col", 0, 0, tiled=False)
    start = lax.axis_index("col") * part_count
    my_frame = lax.dynamic_slice_in_dim(query_frame, start, part_count, 0)
    my_single = lax.dynamic_slice_in_dim(query_single, start, part_count, 0)
    split_out = w_out.reshape(head_count, -1, width)
    w_flat = jnp.concatenate(
        [
            split_out[:, :head_dim].reshape(-1, width),
            split_out[:, head_dim + channels :]
            .reshape(head_count, 3, value_points, width)
            .transpose(1, 0, 2, 3)
            .reshape(-1, width),
        ],
        axis=0,
    )
    w_pair = split_out[:, head_dim : head_dim + channels].reshape(-1, width)
    spread_rows = finish(
        sums, owner, my_frame, my_single, w_pair, w_flat, ln_gain[None, :]
    )
    single_out = lax.all_to_all(spread_rows, "col", 0, 0, tiled=False).reshape(row_count, width)
    return (pair_out, single_out)


def solution(mesh):
    return jax.shard_map(
        per_device,
        mesh=mesh,
        in_specs=(
            P(None, "row", "col"),
            P(),
            P(),
            P("col", None),
            P(None, "col"),
            P(None, "col"),
            P("col"),
            P("col"),
            P(),
            P(),
            P(),
            P(),
            P(),
            P(),
            P(),
            P(),
            P(),
            P(),
        ),
        out_specs=(P(None, "row", "col"), P("row", None)),
        check_vma=False,
    )
```

profile of v0, /device:TPU:4, one launch (start us, length us, event | category | flops | bytes accessed | tf_op | source)
XLA Modules:
  0.0 116.1 jit_solution(8642387882864145696)
XLA Ops:
  0.7 1.3 %dynamic_slice.15 = s32[1,1]{1,0:T(1,128)} dynamic-slice(s32[32,8]{1,0:T(8,128)} %constant.58.clone, s32[]{:T(128)S(6)} %select_n.18, s32[]{:T(128)S(6)} %select_n.19), dynamic_slice_sizes={1,1} | dynamic-slice | bytes 12 | tf_op jit(solution)/shard_map/dynamic_slice | solution.py:561
  4.1 0.8 constant_dynamic-slice_fusion.1
  5.0 2.7 %collective-permute-start.4 = (bf16[88,384]{1,0:T(8,128)(2,1)S(1)}, bf16[88,384]{1,0:T(8,128)(2,1)S(1)}, u32[]{:S(2)}, u32[]{:S(2)}) collective-permute-start(bf16[88,384]{1,0:T(8,128)(2,1)S(1)} %pad_maximum_fusion.3), channel_id=1, source_target_pairs={{80,0},{120,1},{0,2},{104,3},{216,4},{232,5},{136,6},{224,7},{88,8... | collective-permute-start | bytes 202760 | tf_op jit(solution)/shard_map/ppermute | solution.py:568
  7.7 4.1 %turn.1 = (bf16[64,64,256]{2,1,0:T(8,128)(2,1)}, bf16[8,64,64]{2,1,0:T(8,128)(2,1)}, bf16[8,64,64]{2,1,0:T(8,128)(2,1)}) custom-call(bf16[64,64,256]{2,1,0:T(8,128)(2,1)} %pair_ref.1), custom_call_target="tpu_custom_call" | custom-call | tf_op jit(solution)/shard_map/turn/pallas_call | solution.py:39
  11.8 1.2 %fusion.14 = (bf16[8,64,256]{2,1,0:T(8,128)(2,1)S(1)}, bf16[8,64,256]{2,1,0:T(8,128)(2,1)S(1)}) fusion(bf16[64,64,256]{2,1,0:T(8,128)(2,1)} %get-tuple-element.12.own_ref), kind=kLoop, calls=%fused_computation.77 | loop fusion | bytes 1048576 | tf_op jit(solution)/shard_map/slice | solution.py:575
  13.0 2.6 %collective-permute-start = (bf16[8,64,256]{2,1,0:T(8,128)(2,1)S(1)}, bf16[8,64,256]{2,1,0:T(8,128)(2,1)S(1)}, u32[]{:S(2)}, u32[]{:S(2)}) collective-permute-start(bf16[8,64,256]{2,1,0:T(8,128)(2,1)S(1)} %get-tuple-element.33), channel_id=1, source_target_pairs={{0,8},{8,16},{16,24},{24,32},{32,40},{40,48},{48,56},{56,64},{64,7... | collective-permute-start | bytes 786440 | tf_op jit(solution)/shard_map/ppermute | solution.py:442
  15.6 6.6 %collective-permute-start.1 = (bf16[8,64,256]{2,1,0:T(8,128)(2,1)S(1)}, bf16[8,64,256]{2,1,0:T(8,128)(2,1)S(1)}, u32[]{:S(2)}, u32[]{:S(2)}) collective-permute-start(bf16[8,64,256]{2,1,0:T(8,128)(2,1)S(1)} %get-tuple-element.32), channel_id=1, source_target_pairs={{8,0},{16,8},{24,16},{32,24},{40,32},{48,40},{56,48},{64,56},{72,6... | collective-permute-start | bytes 786440 | tf_op jit(solution)/shard_map/ppermute | solution.py:442
  23.2 0.9 copy.65.w_kvpts_ref
  24.1 0.8 copy.63.w_key_ref
  24.9 0.8 copy.64.w_value_ref
  26.5 0.8 copy.66.w_query_ref
  27.3 0.9 copy.67.w_qpts_ref
  28.3 0.8 copy.69.weight_ref
  31.1 4.6 %keys.1 = (bf16[2,256,512]{2,1,0:T(8,128)(2,1)}, bf16[3,256,512]{2,1,0:T(8,128)(2,1)}, f32[16,256]{1,0:T(8,128)}) custom-call(bf16[256,384]{1,0:T(8,128)(2,1)} %single_ref.1, bf16[384,192]{1,0:T(8,128)(2,1)} %copy.63.w_key_ref, bf16[384,192]{1,0:T(8,128)(2,1)} %copy.64.w_value_ref, bf16[384,432]{1,0:T(8,128)(2,1)} %copy.65.w_kvpts_ref, ...), custom_call_target="tpu_custom_call" | custom-call | tf_op jit(solution)/shard_map/keys/pallas_call | solution.py:273
  38.6 1.8 %rim.1 = (bf16[2,64,64]{2,1,0:T(8,128)(2,1)}, bf16[2,64,64]{2,1,0:T(8,128)(2,1)}) custom-call(bf16[8,64,256]{2,1,0:T(8,128)(2,1)} %copy-done.2, bf16[8,64,256]{2,1,0:T(8,128)(2,1)} %copy-done.3), custom_call_target="tpu_custom_call" | custom-call | tf_op jit(solution)/shard_map/rim/pallas_call | solution.py:66
  40.5 0.8 fusion.15
  41.3 1.3 %collective-permute-start.3 = (bf16[10,64,64]{2,1,0:T(8,128)(2,1)S(1)}, bf16[10,64,64]{2,1,0:T(8,128)(2,1)S(1)}, u32[]{:S(2)}, u32[]{:S(2)}) collective-permute-start(bf16[10,64,64]{2,1,0:T(8,128)(2,1)S(1)} %pad_maximum_fusion.2), channel_id=1, source_target_pairs={{1,0},{2,1},{3,2},{4,3},{5,4},{6,5},{7,6},{9,8},{10,9},{11,10},{12... | collective-permute-start | bytes 245768 | tf_op jit(solution)/shard_map/ppermute | solution.py:442
  42.6 4.6 %collective-permute-start.2 = (bf16[10,64,64]{2,1,0:T(8,128)(2,1)S(1)}, bf16[10,64,64]{2,1,0:T(8,128)(2,1)S(1)}, u32[]{:S(2)}, u32[]{:S(2)}) collective-permute-start(bf16[10,64,64]{2,1,0:T(8,128)(2,1)S(1)} %pad_maximum_fusion.1), channel_id=1, source_target_pairs={{0,1},{1,2},{2,3},{3,4},{4,5},{5,6},{6,7},{8,9},{9,10},{10,11},{11... | collective-permute-start | bytes 245768 | tf_op jit(solution)/shard_map/ppermute | solution.py:442
  47.9 5.5 %base.1.base_ref = f32[64,16,256]{2,1,0:T(8,128)} custom-call(bf16[64,384]{1,0:T(8,128)(2,1)} %slice.90.query_ref, bf16[384,192]{1,0:T(8,128)(2,1)} %copy.66.w_query_ref, bf16[384,144]{1,0:T(8,128)(2,1)} %copy.67.w_qpts_ref, f32[64,16]{1,0:T(8,128)} %pad_bitcast_fusion.1.frame_ref, bf16[3,256,512]{2,1,0:T(8,128)(2,1)} %get-tuple-element.17.key_ref, ...), custom_call_target="tpu_custom_call" | custom-call | tf_op jit(solution)/shard_map/base/pallas_call | solution.py:332
  54.2 28.6 %main.1 = (bf16[64,64,256]{2,1,0:T(8,128)(2,1)}, f32[64,16,128]{2,1,0:T(8,128)}) custom-call(bf16[8,64,256]{2,1,0:T(8,128)(2,1)} %copy-done.2, bf16[64,64,256]{2,1,0:T(8,128)(2,1)} %get-tuple-element.12.own_ref, bf16[8,64,256]{2,1,0:T(8,128)(2,1)} %copy-done.3, bf16[10,64,64]{2,1,0:T(8,128)(2,1)} %copy-done.6, bf16[10,64,64]{2,1,0:T(8,128)(2,1)} %copy-done.5, ...), custom_call_target="tpu_custom_call" | custom-call | tf_op jit(solution)/shard_map/main/pallas_call | solution.py:171
  82.8 9.2 %all-to-all-start = ((f32[8,8,16,128]{3,2,1,0:T(8,128)}), f32[8,8,16,128]{3,2,1,0:T(8,128)S(1)}, u32[]{:S(2)}, u32[]{:S(2)}) async-start(f32[8,8,16,128]{3,2,1,0:T(8,128)} %bitcast.52), calls=%async_computation | async-start | bytes 1048576 | tf_op jit(solution)/shard_map/all_to_all | solution.py:645
  92.0 1.0 slice_bitcast_fusion
  92.9 0.9 slice.96
  93.9 2.1 %slice.95 = bf16[12,64,384]{2,1,0:T(8,128)(2,1)} slice(bf16[12,104,384]{2,1,0:T(8,128)(2,1)} %bitcast.48), slice={[0:12], [16:80], [0:384]} | slice | bytes 1179648 | tf_op jit(solution)/shard_map/slice | solution.py:660
  96.6 0.8 pad_maximum_fusion.w_flat_ref
  98.0 1.3 %constant_dynamic-slice_fusion.single_ref = bf16[8,384]{1,0:T(8,128)(2,1)} fusion(bf16[64,384]{1,0:T(8,128)(2,1)} %slice.90.query_ref, s32[]{:T(128)S(6)} %select_n.22), kind=kLoop, calls=%fused_computation.49 | loop fusion | bytes 12292 | tf_op jit(solution)/shard_map/dynamic_slice | solution.py:648
  99.3 1.0 all-to-all-done.sums_ref
  100.2 0.8 copy-done.1
  101.1 3.4 %finish.1 = bf16[8,8,384]{2,1,0:T(8,128)(2,1)} custom-call(f32[8,8,16,128]{3,2,1,0:T(8,128)} %copy-done.1, f32[16,512]{1,0:T(8,128)} %constant.65.clone.owner_ref, f32[8,16]{1,0:T(8,128)} %fusion.12.frame_ref, bf16[8,384]{1,0:T(8,128)(2,1)} %constant_dynamic-slice_fusion.single_ref, bf16[768,384]{1,0:T(8,128)(2,1)} %bitcast.44, ...), custom_call_target="tpu_custom_call" | custom-call | tf_op jit(solution)/shard_map/finish/pallas_call | solution.py:396
  104.5 4.7 %all-to-all-start.1 = ((bf16[8,8,384]{2,1,0:T(8,128)(2,1)}), bf16[8,8,384]{2,1,0:T(8,128)(2,1)S(1)}, u32[]{:S(2)}, u32[]{:S(2)}) async-start(bf16[8,8,384]{2,1,0:T(8,128)(2,1)} %finish.1), calls=%async_computation.1 | async-start | bytes 98304 | tf_op jit(solution)/shard_map/all_to_all | solution.py:664
  109.2 2.5 %copy.72 = bf16[64,64,256]{2,1,0:T(8,128)(2,1)} copy(bf16[64,64,256]{2,0,1:T(8,128)(2,1)S(1)} %bitcast.45) | data formatting | bytes 4194304
  111.7 3.8 %all-to-all-done.1 = bf16[8,8,384]{2,1,0:T(8,128)(2,1)S(1)} async-done(((bf16[8,8,384]{2,1,0:T(8,128)(2,1)}), bf16[8,8,384]{2,1,0:T(8,128)(2,1)S(1)}, u32[]{:S(2)}, u32[]{:S(2)}) %all-to-all-start.1) | async-done | bytes 49184 | tf_op jit(solution)/shard_map/all_to_all | solution.py:664
  (100 shorter events, 11.4 us)
Async XLA Ops:
  0.6 21.6 %copy-start.14 = (f32[3,256]{1,0:T(4,128)S(1)}, f32[3,256]{1,0:T(4,128)}, u32[]{:S(2)}) copy-start(f32[3,256]{1,0:T(4,128)} %param.30) | copy-start | bytes 9220
  0.6 21.7 %copy-start.16 = (f32[3,256]{1,0:T(4,128)S(1)}, f32[3,256]{1,0:T(4,128)}, u32[]{:S(2)}) copy-start(f32[3,256]{1,0:T(4,128)} %param.31) | copy-start | bytes 9220
  0.7 22.5 %copy-start.4 = (bf16[384,432]{0,1:T(8,128)(2,1)S(1)}, bf16[384,432]{0,1:T(8,128)(2,1)}, u32[]{:S(2)}) copy-start(bf16[384,432]{0,1:T(8,128)(2,1)} %param.38) | copy-start | bytes 995332
  5.0 19.1 %copy-start.8 = (bf16[384,192]{0,1:T(8,128)(2,1)S(1)}, bf16[384,192]{0,1:T(8,128)(2,1)}, u32[]{:S(2)}) copy-start(bf16[384,192]{0,1:T(8,128)(2,1)} %param.35) | copy-start | bytes 442372
  5.0 20.0 %copy-start.9 = (bf16[384,192]{0,1:T(8,128)(2,1)S(1)}, bf16[384,192]{0,1:T(8,128)(2,1)}, u32[]{:S(2)}) copy-start(bf16[384,192]{0,1:T(8,128)(2,1)} %param.36) | copy-start | bytes 442372
  5.0 20.8 %copy-start.23 = (f32[12]{0:T(128)S(1)}, f32[12]{0:T(128)}, u32[]{:S(2)}) copy-start(f32[12]{0:T(128)} %param.40) | copy-start | bytes 148
  5.0 20.8 %copy-start.22 = (f32[12]{0:T(128)S(1)}, f32[12]{0:T(128)}, u32[]{:S(2)}) copy-start(f32[12]{0:T(128)} %param.41) | copy-start | bytes 148
  5.0 21.5 %copy-start.20 = (s32[256]{0:T(256)S(1)}, s32[256]{0:T(256)}, u32[]{:S(2)}) copy-start(s32[256]{0:T(256)} %param.33) | copy-start | bytes 3076
  5.0 21.5 %copy-start.10 = (bf16[384,192]{0,1:T(8,128)(2,1)S(1)}, bf16[384,192]{0,1:T(8,128)(2,1)}, u32[]{:S(2)}) copy-start(bf16[384,192]{0,1:T(8,128)(2,1)} %param.34) | copy-start | bytes 442372
  5.0 31.3 %collective-permute-start.4 = (bf16[88,384]{1,0:T(8,128)(2,1)S(1)}, bf16[88,384]{1,0:T(8,128)(2,1)S(1)}, u32[]{:S(2)}, u32[]{:S(2)}) collective-permute-start(bf16[88,384]{1,0:T(8,128)(2,1)S(1)} %pad_maximum_fusion.3), channel_id=1, source_target_pairs={{80,0},{120,1},{0,2},{104,3},{216,4},{232,5},{136,6},{224,7},{88,8... | collective-permute-start | bytes 202760 | tf_op jit(solution)/shard_map/ppermute | solution.py:568
  11.8 15.6 %copy-start.13 = (bf16[384,144]{0,1:T(8,128)(2,1)S(1)}, bf16[384,144]{0,1:T(8,128)(2,1)}, u32[]{:S(2)}) copy-start(bf16[384,144]{0,1:T(8,128)(2,1)} %param.37) | copy-start | bytes 331780
  11.8 16.4 %copy-start.7 = (bf16[9,64,64]{2,1,0:T(8,128)(2,1)S(1)}, bf16[9,64,64]{2,1,0:T(8,128)(2,1)}, u32[]{:S(2)}) copy-start(bf16[9,64,64]{2,1,0:T(8,128)(2,1)} %param.27) | copy-start | bytes 221188
  11.8 17.4 %copy-start.21 = (f32[64]{0:T(128)S(1)}, f32[64]{0:T(128)}, u32[]{:S(2)}) copy-start(f32[64]{0:T(128)} %param.28) | copy-start | bytes 772
  11.8 18.0 %copy-start.15 = (f32[16,256]{1,0:T(8,128)S(1)}, f32[16,256]{1,0:T(8,128)}, u32[]{:S(2)}) copy-start(f32[16,256]{1,0:T(8,128)} %constant.64.clone) | copy-start | bytes 49156
  11.8 18.1 %copy-start.17 = (f32[16,256]{1,0:T(8,128)S(1)}, f32[16,256]{1,0:T(8,128)}, u32[]{:S(2)}) copy-start(f32[16,256]{1,0:T(8,128)} %constant.63.clone) | copy-start | bytes 49156
  11.8 18.7 %copy-start.18 = (bf16[12,64]{1,0:T(8,128)(2,1)S(1)}, bf16[12,64]{1,0:T(8,128)(2,1)}, u32[]{:S(2)}) copy-start(bf16[12,64]{1,0:T(8,128)(2,1)} %param.39) | copy-start | bytes 4612
  13.0 24.2 %collective-permute-start = (bf16[8,64,256]{2,1,0:T(8,128)(2,1)S(1)}, bf16[8,64,256]{2,1,0:T(8,128)(2,1)S(1)}, u32[]{:S(2)}, u32[]{:S(2)}) collective-permute-start(bf16[8,64,256]{2,1,0:T(8,128)(2,1)S(1)} %get-tuple-element.33), channel_id=1, source_target_pairs={{0,8},{8,16},{16,24},{24,32},{32,40},{40,48},{48,56},{56,64},{64,7... | collective-permute-start | bytes 786440 | tf_op jit(solution)/shard_map/ppermute | solution.py:442
  15.6 21.6 %collective-permute-start.1 = (bf16[8,64,256]{2,1,0:T(8,128)(2,1)S(1)}, bf16[8,64,256]{2,1,0:T(8,128)(2,1)S(1)}, u32[]{:S(2)}, u32[]{:S(2)}) collective-permute-start(bf16[8,64,256]{2,1,0:T(8,128)(2,1)S(1)} %get-tuple-element.32), channel_id=1, source_target_pairs={{8,0},{16,8},{24,16},{32,24},{40,32},{48,40},{56,48},{64,56},{72,6... | collective-permute-start | bytes 786440 | tf_op jit(solution)/shard_map/ppermute | solution.py:442
  26.5 14.7 %copy-start.12 = (bf16[8,64,64]{2,1,0:T(8,128)(2,1)S(1)}, bf16[8,64,64]{2,1,0:T(8,128)(2,1)}, u32[]{:S(2)}) copy-start(bf16[8,64,64]{2,1,0:T(8,128)(2,1)} %get-tuple-element.16) | copy-start | bytes 196612
  27.3 15.2 %copy-start.11 = (bf16[8,64,64]{2,1,0:T(8,128)(2,1)S(1)}, bf16[8,64,64]{2,1,0:T(8,128)(2,1)}, u32[]{:S(2)}) copy-start(bf16[8,64,64]{2,1,0:T(8,128)(2,1)} %get-tuple-element.14) | copy-start | bytes 196612
  37.2 0.7 copy-start.2
  37.9 0.7 copy-start.3
  41.3 12.2 %collective-permute-start.3 = (bf16[10,64,64]{2,1,0:T(8,128)(2,1)S(1)}, bf16[10,64,64]{2,1,0:T(8,128)(2,1)S(1)}, u32[]{:S(2)}, u32[]{:S(2)}) collective-permute-start(bf16[10,64,64]{2,1,0:T(8,128)(2,1)S(1)} %pad_maximum_fusion.2), channel_id=1, source_target_pairs={{1,0},{2,1},{3,2},{4,3},{5,4},{6,5},{7,6},{9,8},{10,9},{11,10},{12... | collective-permute-start | bytes 245768 | tf_op jit(solution)/shard_map/ppermute | solution.py:442
  42.6 10.8 %collective-permute-start.2 = (bf16[10,64,64]{2,1,0:T(8,128)(2,1)S(1)}, bf16[10,64,64]{2,1,0:T(8,128)(2,1)S(1)}, u32[]{:S(2)}, u32[]{:S(2)}) collective-permute-start(bf16[10,64,64]{2,1,0:T(8,128)(2,1)S(1)} %pad_maximum_fusion.1), channel_id=1, source_target_pairs={{0,1},{1,2},{2,3},{3,4},{4,5},{5,6},{6,7},{8,9},{9,10},{10,11},{11... | collective-permute-start | bytes 245768 | tf_op jit(solution)/shard_map/ppermute | solution.py:442
  53.4 0.7 copy-start.5
  53.5 0.7 copy-start.6
  82.8 13.2 %copy-start.19 = (f32[384]{0:T(512)S(1)}, f32[384]{0:T(512)}, u32[]{:S(2)}) copy-start(f32[384]{0:T(512)} %param.43) | copy-start | bytes 4612
  82.8 17.4 %all-to-all-start = ((f32[8,8,16,128]{3,2,1,0:T(8,128)}), f32[8,8,16,128]{3,2,1,0:T(8,128)S(1)}, u32[]{:S(2)}, u32[]{:S(2)}) async-start(f32[8,8,16,128]{3,2,1,0:T(8,128)} %bitcast.52), calls=%async_computation | async-start | bytes 1048576 | tf_op jit(solution)/shard_map/all_to_all | solution.py:645
  93.9 15.4 %copy-start = (bf16[64,64,256]{2,1,0:T(8,128)(2,1)S(1)}, bf16[64,64,256]{2,1,0:T(8,128)(2,1)}, u32[]{:S(2)}) copy-start(bf16[64,64,256]{2,1,0:T(8,128)(2,1)} %get-tuple-element.20) | copy-start | bytes 6291460
  100.2 0.8 copy-start.1
  104.5 11.0 %all-to-all-start.1 = ((bf16[8,8,384]{2,1,0:T(8,128)(2,1)}), bf16[8,8,384]{2,1,0:T(8,128)(2,1)S(1)}, u32[]{:S(2)}, u32[]{:S(2)}) async-start(bf16[8,8,384]{2,1,0:T(8,128)(2,1)} %finish.1), calls=%async_computation.1 | async-start | bytes 98304 | tf_op jit(solution)/shard_map/all_to_all | solution.py:664
where the time goes:
time: 117 us; the launch traced here: 116 us
  Pallas kernels  48.1 us (41%)
  starting transfers between devices  31.7 us (27%)
  local copies, waits for them, and re-layouts  26 us (22%)
  waiting for transfers between devices  4.8 us (4%)
  other arithmetic  3.79 us (3%)
  between operations  1.73 us (1%)
    pallas_call x1, Pallas kernels, main(): pl.pallas_call(main_kernel, grid=(steps,), in_specs=[pl.BlockSpec(up.shap...  28.6 us
    ppermute x4, starting transfers between devices, shifted(): return lax.ppermute(cells, axis, routes)  15.1 us
    unnamed x55, local copies, waits for them, and re-layouts  10.4 us
    all_to_all x1, starting transfers between devices, per_device(): sums = lax.all_to_all(sums, 'col', 0, 0, tiled=False)  9.16 us
    pallas_call x1, Pallas kernels, base_logits(): pl.pallas_call(base_kernel, grid=(count // step,), in_specs=[pl.BlockSpec...  5.54 us
    all_to_all x1, starting transfers between devices, per_device(): lax.all_to_all(spread_rows, 'col', 0, 0, tiled=False)  4.72 us
    pallas_call x1, Pallas kernels, keys(): pl.pallas_call(keys_kernel, out_shape=[jax.ShapeDtypeStruct((2, count, 51...  4.59 us
    pallas_call x1, Pallas kernels, turn(): pl.pallas_call(turn_kernel, grid=(row_count // step,), in_specs=[pl.Block...  4.06 us
  transfers between devices with their start and end apart: 7, of which 2 were waited for; matrix products, arithmetic and copies ran while one was open for 19% of the time, Pallas kernels for 12%

commit v1 on v0

v1 whole, which is shorter than its diff:
```python
import math

import jax
import jax.numpy as jnp
import numpy as np
from jax import lax
from jax.experimental import pallas as pl
from jax.experimental.pallas import tpu as pltpu
from jax.sharding import PartitionSpec as P

DILATION_STEP = 8


logit_scale = math.sqrt(1.0 / 3.0)
mask_penalty = 10000.0
norm_eps = 1e-05
highest = lax.Precision.HIGHEST


def in_pieces(value, count):
    parts = []
    for _ in range(count - 1):
        part = value.astype(jnp.bfloat16)
        parts.append(part)
        value = value - part.astype(jnp.float32)
    parts.append(value.astype(jnp.bfloat16))
    return parts


def dot32(a, b):
    return jnp.dot(a, b, preferred_element_type=jnp.float32)


def dot32_nt(a, b):
    return lax.dot_general(a, b, (((1,), (1,)), ((), ())), preferred_element_type=jnp.float32)


def edge_cells(rows):
    head = jnp.concatenate([row[:, :DILATION_STEP] for row in rows], axis=1)
    tail = jnp.concatenate([row[:, row.shape[1] - DILATION_STEP :] for row in rows], axis=1)
    return head, tail


def turn_kernel(pair_ref, rows_ref, head_ref, tail_ref):
    turned = jnp.swapaxes(pair_ref[...], 0, 1)
    rows_ref[...] = turned
    for block in range(turned.shape[0] // 8):
        head, tail = edge_cells([turned[8 * block + i] for i in range(8)])
        head_ref[block] = head
        tail_ref[block] = tail


def turn(pair):
    channels, row_count, col_count = pair.shape
    step = 16
    edge = jax.ShapeDtypeStruct((row_count // 8, channels, 64), pair.dtype)
    return pl.pallas_call(
        turn_kernel,
        grid=(row_count // step,),
        in_specs=[pl.BlockSpec((channels, step, col_count), lambda b: (0, b, 0))],
        out_specs=[
            pl.BlockSpec((step, channels, col_count), lambda b: (b, 0, 0)),
            pl.BlockSpec((step // 8, channels, 64), lambda b: (b, 0, 0)),
            pl.BlockSpec((step // 8, channels, 64), lambda b: (b, 0, 0)),
        ],
        out_shape=[
            jax.ShapeDtypeStruct((row_count, channels, col_count), pair.dtype),
            edge,
            edge,
        ],
        name="turn",
    )(pair)


def rim_kernel(raw_up_ref, raw_down_ref, up_ref, down_ref, head_ref, tail_ref):
    for index, (raw, ref) in enumerate(((raw_up_ref, up_ref), (raw_down_ref, down_ref))):
        turned = jnp.swapaxes(raw[...], 0, 1)
        ref[...] = turned
        head, tail = edge_cells([turned[i] for i in range(8)])
        head_ref[index] = head
        tail_ref[index] = tail


def rim(raw_up, raw_down):
    channels, count, cols = raw_up.shape
    rows = jax.ShapeDtypeStruct((count, channels, cols), raw_up.dtype)
    edge = jax.ShapeDtypeStruct((2, channels, 64), raw_up.dtype)
    return pl.pallas_call(rim_kernel, out_shape=[rows, rows, edge, edge], name="rim")(
        raw_up, raw_down
    )


def as_column(row, count):
    shape = (count, row.shape[1])
    same = lax.broadcasted_iota(jnp.int32, shape, 0) == lax.broadcasted_iota(jnp.int32, shape, 1)
    return jnp.sum(jnp.where(same, row, 0.0), axis=1, keepdims=True)


def frame_columns(rows):
    comp_b, comp_c, comp_d = rows[0:1], rows[1:2], rows[2:3]
    bb, cc, dd = comp_b * comp_b, comp_c * comp_c, comp_d * comp_d
    inverse = 1.0 / (1.0 + bb + cc + dd)
    turned = [
        1.0 + bb - cc - dd,
        2.0 * (comp_b * comp_c - comp_d),
        2.0 * (comp_b * comp_d + comp_c),
        2.0 * (comp_b * comp_c + comp_d),
        1.0 - bb + cc - dd,
        2.0 * (comp_c * comp_d - comp_b),
        2.0 * (comp_b * comp_d - comp_c),
        2.0 * (comp_c * comp_d + comp_b),
        1.0 - bb - cc + dd,
    ]
    count = rows.shape[1]
    stacked = jnp.concatenate(
        [part * inverse for part in turned]
        + [rows[3:7], jnp.zeros((3, count), jnp.float32)],
        axis=0,
    )
    shape = (count, count)
    same = lax.broadcasted_iota(jnp.int32, shape, 0) == lax.broadcasted_iota(jnp.int32, shape, 1)
    eye = same.astype(jnp.bfloat16)
    columns = jnp.zeros((count, 16), jnp.float32)
    for part in in_pieces(stacked, 3):
        columns = columns + dot32_nt(eye, part)
    return columns


def main_kernel(
    up_ref,
    own_ref,
    down_ref,
    left_ref,
    right_ref,
    taps_ref,
    params_ref,
    raw_bias_ref,
    base_ref,
    value_ref,
    owner_ref,
    out_ref,
    sums_ref,
    window_ref,
    soft_ref,
    weight_ref,
    head_bias_ref,
    shift_ref,
):
    step = pl.program_id(0)
    last = pl.num_programs(0) - 1
    channels = own_ref.shape[1]
    cols = own_ref.shape[2]
    slot = lax.rem(step, 3)

    def stage(source):
        lane = lax.broadcasted_iota(jnp.int32, (channels, 128), 1)
        empty = jnp.zeros((channels, 64), jnp.bfloat16)
        before = jnp.concatenate([left_ref[0], empty], axis=1)
        after = jnp.concatenate([right_ref[0], empty], axis=1)
        top = channels
        for i in range(8):
            cells = source[i]
            ahead = [pltpu.roll(cells[:, 128 * k : 128 * k + 128], 8, 1) for k in range(2)]
            fill = pltpu.roll(before, (128 - 8 * i) % 128, 1)
            window_ref[slot, i, 0:top, 0:128] = jnp.where(lane < 8, fill, ahead[0])
            window_ref[slot, i, 0:top, 128:256] = jnp.where(lane < 8, ahead[0], ahead[1])
            window_ref[slot, i, top : 2 * top] = cells
            back = [pltpu.roll(cells[:, 128 * k : 128 * k + 128], 120, 1) for k in range(2)]
            fill = pltpu.roll(after, 120 - 8 * i, 1)
            window_ref[slot, i, 2 * top : 3 * top, 0:128] = jnp.where(lane >= 120, back[1], back[0])
            window_ref[slot, i, 2 * top : 3 * top, 128:256] = jnp.where(lane >= 120, fill, back[1])

    @pl.when(step == 0)
    def _():
        for dy in range(3):
            weight_ref[dy] = jnp.concatenate([taps_ref[3 * dy + dx] for dx in range(3)], axis=1)
        heads = raw_bias_ref.shape[0]
        pick = lax.broadcasted_iota(jnp.int32, (16, heads), 0) == lax.broadcasted_iota(
            jnp.int32, (16, heads), 1
        )
        head_bias_ref[...] = dot32(pick.astype(jnp.bfloat16), raw_bias_ref[...]).astype(jnp.bfloat16)
        shift_ref[...] = jnp.broadcast_to(as_column(params_ref[1:2, :], channels), (channels, cols))
        stage(up_ref)

    @pl.when(jnp.logical_and(step > 0, step < last))
    def _():
        stage(own_ref)

    @pl.when(step == last)
    def _():
        stage(down_ref)

    @pl.when(step >= 2)
    def _():
        first = lax.rem(step + 1, 3)
        middle = lax.rem(step + 2, 3)
        lane = lax.broadcasted_iota(jnp.int32, (8, 16, 128), 2)

        def convolve(i):
            return (
                jnp.dot(weight_ref[0], window_ref[first, i], preferred_element_type=jnp.float32)
                + jnp.dot(weight_ref[1], window_ref[middle, i], preferred_element_type=jnp.float32)
                + jnp.dot(weight_ref[2], window_ref[slot, i], preferred_element_type=jnp.float32)
            )

        shift = shift_ref[...]
        pending = convolve(0)
        for i in range(8):
            conv = pending + shift
            if i < 7:
                pending = convolve(i + 1)
            bent = jnp.where(conv > 0.0, conv, jnp.exp(jnp.minimum(conv, 0.0)) - 1.0)
            cells = window_ref[middle, i, channels : 2 * channels].astype(jnp.float32)
            out_ref[i] = (cells + bent).astype(jnp.bfloat16)
        bias = jnp.stack(
            [
                jnp.dot(head_bias_ref[...], out_ref[i], preferred_element_type=jnp.float32)
                for i in range(8)
            ]
        )
        logits = base_ref[...] + logit_scale * bias
        peak = jnp.max(logits, axis=2, keepdims=True)
        weights = jnp.exp(logits - peak).astype(jnp.bfloat16)
        total = jnp.sum(weights.astype(jnp.float32), axis=2, keepdims=True)
        pair_sum = jnp.stack(
            [
                lax.dot_general(
                    weights[i],
                    out_ref[i],
                    (((1,), (1,)), ((), ())),
                    preferred_element_type=jnp.float32,
                )
                for i in range(8)
            ]
        )
        padded = jnp.concatenate([pair_sum, jnp.zeros((8, 16, 64), jnp.float32)], axis=2)
        row = pl.multiple_of((step - 2) * 8, 8)
        sums_ref[pl.ds(row, 8)] = jnp.where(
            lane == 104, peak, jnp.where(lane == 105, total, padded)
        )
        soft_ref[pl.ds(pl.multiple_of(row * 16, 128), 128), :] = weights.reshape(128, cols)

    @pl.when(step == last)
    def _():
        chunk = 256
        sub = lax.broadcasted_iota(jnp.int32, (chunk // 16, 16, 128), 1)
        for part in range(soft_ref.shape[0] // chunk):
            soft = soft_ref[part * chunk : (part + 1) * chunk, :]
            acc = jnp.dot(soft, value_ref[0], preferred_element_type=jnp.float32) + jnp.dot(
                soft, value_ref[1], preferred_element_type=jnp.float32
            )
            acc = acc.reshape(chunk // 16, 16, 512) * owner_ref[...][None]
            folded = jnp.sum(acc, axis=1, keepdims=True)
            rows = slice(part * chunk // 16, (part + 1) * chunk // 16)
            kept = sums_ref[rows]
            for k in range(4):
                lanes = folded[:, :, 128 * k : 128 * k + 128]
                kept = jnp.where(sub == 12 + k, lanes, kept)
            sums_ref[rows] = kept


def main(up, own, down, left, right, weight, bias, head_bias, base, value, owner):
    row_count, channels, col_count = own.shape
    steps = row_count // 8 + 2
    fixed3 = lambda b: (0, 0, 0)
    fixed2 = lambda b: (0, 0)
    late = lambda b: (jnp.maximum(b - 2, 0), 0, 0)
    return pl.pallas_call(
        main_kernel,
        grid=(steps,),
        in_specs=[
            pl.BlockSpec(up.shape, fixed3),
            pl.BlockSpec((8, channels, col_count), lambda b: (jnp.clip(b - 1, 0, steps - 3), 0, 0)),
            pl.BlockSpec(down.shape, fixed3),
            pl.BlockSpec((1, channels, 64), lambda b: (b, 0, 0)),
            pl.BlockSpec((1, channels, 64), lambda b: (b, 0, 0)),
            pl.BlockSpec(weight.shape, fixed3),
            pl.BlockSpec(bias.shape, fixed2),
            pl.BlockSpec(head_bias.shape, fixed2),
            pl.BlockSpec((8, 16, col_count), late),
            pl.BlockSpec(value.shape, fixed3),
            pl.BlockSpec(owner.shape, fixed2),
        ],
        out_specs=[
            pl.BlockSpec((8, channels, col_count), late),
            pl.BlockSpec((row_count, 16, 128), fixed3),
        ],
        out_shape=[
            jax.ShapeDtypeStruct((row_count, channels, col_count), jnp.bfloat16),
            jax.ShapeDtypeStruct((row_count, 16, 128), jnp.float32),
        ],
        scratch_shapes=[
            pltpu.VMEM((3, 8, 3 * channels, col_count), jnp.bfloat16),
            pltpu.VMEM((row_count * 16, col_count), jnp.bfloat16),
            pltpu.VMEM((3, channels, 3 * channels), jnp.bfloat16),
            pltpu.VMEM((16, channels), jnp.bfloat16),
            pltpu.VMEM((channels, col_count), jnp.float32),
        ],
        name="main",
    )(up, own, down, left, right, weight, bias, head_bias, base, value, owner)


def to_global(local, frame):
    span = local.shape[1] // 3
    turned = []
    for x in range(3):
        total = frame[:, 9 + x : 10 + x]
        for d in range(3):
            column = frame[:, 3 * x + d : 3 * x + d + 1]
            total = total + column * local[:, span * d : span * (d + 1)]
        turned.append(total)
    return jnp.concatenate(turned, axis=1)


def keys_kernel(
    single_ref,
    w_key_ref,
    w_value_ref,
    w_kvpts_ref,
    frame_ref,
    pick_key_ref,
    pick_value_ref,
    shift_value_ref,
    points_ref,
    value_ref,
    key_ref,
    key_sq_ref,
):
    rows = single_ref[...]
    key = dot32_nt(rows, w_key_ref[...])
    value = dot32_nt(rows, w_value_ref[...]).astype(jnp.bfloat16)
    points = to_global(dot32_nt(rows, w_kvpts_ref[...]), frame_columns(frame_ref[...]))
    point_parts = in_pieces(points, 3)
    key_parts = in_pieces(
        jnp.concatenate([key, jnp.zeros((key.shape[0], 256 - key.shape[1]), jnp.float32)], axis=1), 3
    )
    whole = jnp.zeros((rows.shape[0], 256), jnp.float32)
    for index in range(3):
        picked = dot32(point_parts[index], pick_key_ref[...])
        whole = whole + picked
        key_ref[index, :, 0:256] = key_parts[index]
        key_ref[index, :, 256:512] = picked.astype(jnp.bfloat16)
    square = jnp.zeros((16, rows.shape[0]), jnp.float32)
    for part in in_pieces(whole * whole, 3):
        square = square + dot32_nt(points_ref[...], part)
    key_sq_ref[...] = square
    value_ref[0] = (
        dot32(value, shift_value_ref[...]) + dot32(point_parts[0], pick_value_ref[...])
    ).astype(jnp.bfloat16)
    value_ref[1] = dot32(point_parts[1], pick_value_ref[...]).astype(jnp.bfloat16)


def keys(single, w_key, w_value, w_kvpts, frame, pick_key, pick_value, shift_value, points):
    count = single.shape[0]
    return pl.pallas_call(
        keys_kernel,
        out_shape=[
            jax.ShapeDtypeStruct((2, count, 512), jnp.bfloat16),
            jax.ShapeDtypeStruct((3, count, 512), jnp.bfloat16),
            jax.ShapeDtypeStruct((16, count), jnp.float32),
        ],
        name="keys",
    )(single, w_key, w_value, w_kvpts, frame, pick_key, pick_value, shift_value, points)


def base_kernel(
    query_ref,
    w_query_ref,
    w_qpts_ref,
    key_ref,
    key_sq_ref,
    table_ref,
    params_ref,
    key_row_ref,
    base_ref,
    frame_ref,
):
    step = pl.program_id(0)
    count = base_ref.shape[0]

    @pl.when(step == 0)
    def _():
        every = query_ref.shape[0] - 24
        tail = query_ref[every:, 0:every].astype(jnp.float32)
        frame_ref[...] = frame_columns(tail[0:8] + tail[8:16] + tail[16:24])

    own = pl.ds(pl.multiple_of(step * count, count), count)
    rows = query_ref[own, :]
    frame = frame_ref[own, :]
    query = dot32_nt(rows, w_query_ref[...])
    points = to_global(dot32_nt(rows, w_qpts_ref[...]), frame)
    points = jnp.concatenate([points, jnp.zeros((count, 256 - points.shape[1]), jnp.float32)], axis=1)
    query = jnp.concatenate([query, jnp.zeros((count, 256 - query.shape[1]), jnp.float32)], axis=1)
    point_scale = as_column(params_ref[2:3, :], 16)
    query = query[:, None, :] * table_ref[:, 0:256][None]
    scaled = points[:, None, :] * (table_ref[:, 256:512] * point_scale)[None]
    own_sq = 0.5 * jnp.sum(scaled * points[:, None, :], axis=2, keepdims=True)
    query_parts = in_pieces(query.reshape(count * 16, 256), 3)
    point_parts = in_pieces(scaled.reshape(count * 16, 256), 3)
    total = jnp.zeros((count * 16, key_ref.shape[1]), jnp.float32)
    for a, b in ((2, 0), (1, 1), (0, 2), (1, 0), (0, 1), (0, 0)):
        total = total + dot32_nt(
            jnp.concatenate([query_parts[a], point_parts[a]], axis=1), key_ref[b]
        )
    scale = 0.5 * point_scale
    chain = as_column(params_ref[3:4, :], 16)
    same = (frame[:, 12:13] == key_row_ref[6:7, :]).astype(jnp.float32)
    shared = scale * key_sq_ref[...]
    base_ref[...] = (
        total.reshape(count, 16, -1)
        - own_sq
        - shared[None]
        + chain[None] * same[:, None, :]
        - key_row_ref[7:8, :][None]
    )


def base_logits(query, w_query, w_qpts, key, key_sq, table, params, key_row):
    count = query.shape[0] - 24
    step = 16
    whole2 = lambda b: (0, 0)
    whole3 = lambda b: (0, 0, 0)
    operands = (query, w_query, w_qpts, key, key_sq, table, params, key_row)
    return pl.pallas_call(
        base_kernel,
        grid=(count // step,),
        in_specs=[pl.BlockSpec(x.shape, whole3 if x.ndim == 3 else whole2) for x in operands],
        out_specs=[
            pl.BlockSpec((step, 16, key.shape[1]), whole3_at),
            pl.BlockSpec((count, 16), whole2),
        ],
        out_shape=[
            jax.ShapeDtypeStruct((count, 16, key.shape[1]), jnp.float32),
            jax.ShapeDtypeStruct((count, 16), jnp.float32),
        ],
        name="base",
    )(*operands)


def whole3_at(b):
    return (b, 0, 0)


def finish_kernel(
    sums_ref, owner_ref, frame_ref, message_ref, w_out_ref, params_ref, out_ref
):
    sums = sums_ref[...]
    parts, count = sums.shape[0], sums.shape[1]
    width = message_ref.shape[1]
    place = lax.axis_index("col") * count
    live = lax.broadcasted_iota(jnp.int32, sums.shape[:3] + (1,), 2) < 12
    peaks = jnp.where(live, sums[:, :, :, 104:105], 0.0)
    scales = jnp.exp(peaks - jnp.max(peaks, axis=0, keepdims=True))
    counts = jnp.where(live, sums[:, :, :, 105:106], 1.0)
    totals = jnp.sum(counts * scales, axis=0, keepdims=True)
    scales = scales / totals
    means = jnp.sum(sums * scales, axis=0)
    flats = []
    for k in range(4):
        own = owner_ref[:, 128 * k : 128 * k + 128]
        lanes = jnp.sum(scales * own[None, None], axis=2)
        flats.append(jnp.sum(sums[:, :, 12 + k, :] * lanes, axis=0))
    flat = jnp.concatenate(flats, axis=1)
    frame = frame_ref[pl.ds(pl.multiple_of(place, count), count), :]
    centred = [flat[:, 192 + 96 * x : 288 + 96 * x] - frame[:, 9 + x : 10 + x] for x in range(3)]
    local = [
        sum(frame[:, 3 * x + d : 3 * x + d + 1] * centred[x] for x in range(3)) for d in range(3)
    ]
    features = []
    for h in range(12):
        features += [flat[:, 16 * h : 16 * h + 16], means[:, h, 0:64]]
        features += [part[:, 8 * h : 8 * h + 8] for part in local]
    update = jnp.zeros((count, width), jnp.float32)
    for part in reversed(in_pieces(jnp.concatenate(features, axis=1), 3)):
        update = update + dot32(part, w_out_ref[...])
    shape = (count, message_ref.shape[0])
    mine = lax.broadcasted_iota(jnp.int32, shape, 1) == place + lax.broadcasted_iota(
        jnp.int32, shape, 0
    )
    single = dot32(mine.astype(jnp.bfloat16), message_ref[...])
    hidden = single + update
    row_mean = jnp.mean(hidden, axis=1, keepdims=True)
    row_var = jnp.mean((hidden - row_mean) ** 2, axis=1, keepdims=True)
    rows = ((hidden - row_mean) * lax.rsqrt(row_var + norm_eps) * params_ref[0:1, :]).astype(jnp.bfloat16)
    for index in range(parts):
        out_ref[index] = rows


def finish(sums, owner, frame, message, w_out, params):
    parts, count = sums.shape[:2]
    return pl.pallas_call(
        finish_kernel,
        out_shape=jax.ShapeDtypeStruct((parts, count, message.shape[1]), jnp.bfloat16),
        name="finish",
    )(sums, owner, frame, message, w_out, params)


def pack_kernel(single_ref, rows_ref, message_ref):
    count = message_ref.shape[0] - 24
    width = message_ref.shape[1]
    slots = single_ref.shape[0] // count
    slot = lax.axis_index("row") % slots
    message_ref[0:count, :] = single_ref[pl.ds(pl.multiple_of(slot * count, count), count), :]
    rows = rows_ref[:, 0:count]
    for k in range(1, slots):
        rows = jnp.where(slot == k, rows_ref[:, k * count : (k + 1) * count], rows)
    rows = jnp.concatenate([rows, jnp.zeros((rows.shape[0], width - count), jnp.float32)], axis=1)
    for k, part in enumerate(in_pieces(rows, 3)):
        message_ref[count + 8 * k : count + 8 * k + 8, :] = part


def pack(single, rows, count):
    return pl.pallas_call(
        pack_kernel,
        out_shape=jax.ShapeDtypeStruct((count + 24, single.shape[1]), single.dtype),
        name="pack",
    )(single, rows)


def tables(head_count, head_dim, query_points, value_points):
    both = query_points + value_points
    span = 3 * head_count * both
    pick_key = np.zeros((span, 256), np.float32)
    pick_value = np.zeros((span, 512), np.float32)
    shift_value = np.zeros((head_count * head_dim, 512), np.float32)
    points = np.zeros((16, 256), np.float32)
    scalars = np.zeros((16, 256), np.float32)
    owner = np.zeros((16, 512), np.float32)
    for h in range(head_count):
        for d in range(head_dim):
            lane = h * head_dim + d
            scalars[h, lane] = 1.0
            owner[h, lane] = 1.0
            shift_value[lane, lane] = 1.0
        for x in range(3):
            first = (x * head_count + h) * both
            for p in range(query_points):
                lane = (x * head_count + h) * query_points + p
                pick_key[first + p, lane] = 1.0
                points[h, lane] = 1.0
            for p in range(value_points):
                lane = head_count * head_dim + (x * head_count + h) * value_points + p
                pick_value[first + query_points + p, lane] = 1.0
                owner[h, lane] = 1.0
    return pick_key, pick_value, shift_value, points, scalars, owner


def shifted(cells, axis, forward):
    count = lax.axis_size(axis)
    if forward:
        routes = [(i, i + 1) for i in range(count - 1)]
    else:
        routes = [(i + 1, i) for i in range(count - 1)]
    return lax.ppermute(cells, axis, routes)


def query_routes(n_row, n_col):
    group = n_row // n_col
    pairs = []
    for holder_col in range(n_col):
        for holder in range(n_row):
            slot = holder // group
            half = n_col // 2
            col = slot // half * half + (slot + half // 2) % half
            target = holder_col * group + holder % group
            pairs.append((holder * n_col + holder_col, target * n_col + col))
    return pairs


def per_device(
    pair,
    conv_weight,
    conv_bias,
    single,
    quat_vec,
    trans,
    chain_id,
    residue_mask,
    w_query,
    w_key,
    w_value,
    w_qpts,
    w_kvpts,
    w_bias,
    head_weight,
    chain_weight,
    w_out,
    ln_gain,
):
    channels, row_count, col_count = pair.shape
    head_count = w_bias.shape[0]
    head_dim = w_query.shape[1] // head_count
    width = single.shape[1]
    query_points = w_qpts.shape[1] // (3 * head_count)
    value_points = w_kvpts.shape[1] // (3 * head_count) - query_points
    n_row, n_col = lax.axis_size("row"), lax.axis_size("col")
    part_count = row_count // n_col

    raw_up = shifted(pair[:, row_count - DILATION_STEP :], "row", True)
    raw_down = shifted(pair[:, :DILATION_STEP], "row", False)
    routes = query_routes(n_row, n_col)
    rows = jnp.concatenate(
        [
            quat_vec,
            trans,
            chain_id.astype(jnp.float32)[None, :],
            mask_penalty * (1.0 - residue_mask.astype(jnp.float32))[None, :],
        ],
        axis=0,
    )
    message = lax.ppermute(pack(single, rows, row_count), ("row", "col"), routes)
    point_scale = logit_scale * jax.nn.softplus(head_weight) * math.sqrt(2.0 / (9.0 * query_points))
    wide = lambda row: jnp.pad(row, (0, width - row.shape[0]))[None, :]
    params = jnp.concatenate(
        [wide(ln_gain), wide(conv_bias), wide(point_scale), wide(chain_weight)]
        + [jnp.zeros((4, width), jnp.float32)],
        axis=0,
    )
    own, own_head, own_tail = turn(pair)
    up, down, rim_head, rim_tail = rim(raw_up, raw_down)
    to_right = jnp.concatenate([rim_tail[:1], own_tail, rim_tail[1:]], axis=0)
    to_left = jnp.concatenate([rim_head[:1], own_head, rim_head[1:]], axis=0)
    to_right, to_left, key_rows = lax.optimization_barrier((to_right, to_left, rows))
    left = shifted(to_right, "col", True)
    right = shifted(to_left, "col", False)
    pick_key, pick_value, shift_value, points, scalars, owner = tables(
        head_count, head_dim, query_points, value_points
    )
    value, key, key_sq = keys(
        single,
        w_key.T,
        w_value.T,
        w_kvpts.T,
        key_rows,
        jnp.asarray(pick_key, jnp.bfloat16),
        jnp.asarray(pick_value, jnp.bfloat16),
        jnp.asarray(shift_value, jnp.bfloat16),
        jnp.asarray(points, jnp.bfloat16),
    )
    table = np.concatenate([scalars * (logit_scale / math.sqrt(head_dim)), points], axis=1)
    base, frame = base_logits(
        message,
        w_query.T,
        w_qpts.T,
        key,
        key_sq,
        jnp.asarray(table, jnp.float32),
        params,
        key_rows,
    )
    owner = jnp.asarray(owner, jnp.float32)
    updated, sums = main(
        up,
        own,
        down,
        left,
        right,
        conv_weight,
        params,
        w_bias,
        base,
        value,
        owner,
    )
    pair_out = updated.transpose(1, 0, 2)
    sums = sums.reshape(n_col, part_count, 16, 128)
    sums = lax.all_to_all(sums, "col", 0, 0, tiled=False)
    spread_rows = finish(sums, owner, frame, message, w_out, params)
    single_out = lax.all_to_all(spread_rows, "col", 0, 0, tiled=False).reshape(row_count, width)
    return (pair_out, single_out)


def solution(mesh):
    return jax.shard_map(
        per_device,
        mesh=mesh,
        in_specs=(
            P(None, "row", "col"),
            P(),
            P(),
            P("col", None),
            P(None, "col"),
            P(None, "col"),
            P("col"),
            P("col"),
            P(),
            P(),
            P(),
            P(),
            P(),
            P(),
            P(),
            P(),
            P(),
            P(),
        ),
        out_specs=(P(None, "row", "col"), P("row", None)),
        check_vma=False,
    )
```

time: 117 us -> 92.4 us (0.79)
  local copies, waits for them, and re-layouts: 26 us -> 7.68 us
  blocking collectives: 0 us -> 16.6 us
  starting transfers between devices: 31.7 us -> 15.1 us
  Pallas kernels: 48.1 us -> 36.6 us
  waiting for transfers between devices: 4.8 us -> 9.27 us
    all_to_all x0 -> x1, blocking collectives: none -> 16.6 us  [per_device(): sums = lax.all_to_all(sums, 'col', 0, 0, tiled=False)]
    pallas_call x1, Pallas kernels: 28.6 us -> 14.3 us  [main(): pl.pallas_call(main_kernel, grid=(steps,), in_specs=[pl.BlockSpec(up.shap...]
    all_to_all x1 -> x0, starting transfers between devices: 9.16 us -> none  [per_device(): sums = lax.all_to_all(sums, 'col', 0, 0, tiled=False)]
    ppermute x4, waiting for transfers between devices: 0.01 us -> 5.55 us  [shifted(): return lax.ppermute(cells, axis, routes)]
    unnamed x55 -> x22, local copies, waits for them, and re-layouts: 10.4 us -> 5.19 us
    dynamic_slice x4 -> x0, local copies, waits for them, and re-layouts: 4.01 us -> none  [the longest x1 1.32 us: per_device(): jnp.asarray(offsets)[lax.axis_index('row'), lax.axis_index('col')]]
    slice x6 -> x2, local copies, waits for them, and re-layouts: 5.6 us -> 1.85 us  [the longest x1 1.07 us: per_device(): raw_down = shifted(pair[:, :DILATION_STEP], 'row', False)]
    ppermute x4, starting transfers between devices: 15.1 us -> 11.8 us  [shifted(): return lax.ppermute(cells, axis, routes)]
  transfers between devices with their start and end apart: 7 -> 6, of which waited for: 2 -> 2; matrix products, arithmetic and copies ran while one was open for 19% -> 9% of each run, Pallas kernels for 12% -> 21%
where the time goes in v1:
time: 92.4 us; the launch traced here: 90.8 us
  Pallas kernels  36.6 us (40%)
  blocking collectives  16.6 us (18%)
  starting transfers between devices  15.1 us (16%)
  waiting for transfers between devices  9.27 us (10%)
  local copies, waits for them, and re-layouts  7.68 us (8%)
  other arithmetic  4.58 us (5%)
    all_to_all x1, blocking collectives, per_device(): sums = lax.all_to_all(sums, 'col', 0, 0, tiled=False)  16.6 us
    pallas_call x1, Pallas kernels, main(): pl.pallas_call(main_kernel, grid=(steps,), in_specs=[pl.BlockSpec(up.shap...  14.3 us
    ppermute x4, starting transfers between devices, shifted(): return lax.ppermute(cells, axis, routes)  11.8 us
    pallas_call x1, Pallas kernels, base_logits(): pl.pallas_call(base_kernel, grid=(count // step,), in_specs=[pl.BlockSpec...  5.93 us
    ppermute x4, waiting for transfers between devices, shifted(): return lax.ppermute(cells, axis, routes)  5.55 us
    unnamed x22, local copies, waits for them, and re-layouts  5.19 us
    pallas_call x1, Pallas kernels, keys(): pl.pallas_call(keys_kernel, out_shape=[jax.ShapeDtypeStruct((2, count, 51...  4.98 us
    pallas_call x1, Pallas kernels, turn(): pl.pallas_call(turn_kernel, grid=(row_count // step,), in_specs=[pl.Block...  4.06 us
  transfers between devices with their start and end apart: 6, of which 2 were waited for; matrix products, arithmetic and copies ran while one was open for 9% of the time, Pallas kernels for 21%

profile of v1, /device:TPU:4, one launch (start us, length us, event | category | flops | bytes accessed | tf_op | source)
XLA Modules:
  0.0 90.8 jit_solution(2228480697992762403)
XLA Ops:
  0.6 1.1 %fusion.1 = (bf16[64,8,256]{2,1,0:T(8,128)(2,1)S(1)}, bf16[64,8,256]{2,1,0:T(8,128)(2,1)S(1)}) fusion(bf16[64,64,256]{2,1,0:T(8,128)(2,1)} %pair_ref.1), kind=kLoop, calls=%fused_computation.6 | loop fusion | bytes 1048576 | tf_op jit(solution)/shard_map/slice | solution.py:600
  1.7 0.0 copy-start.9
  1.7 0.0 copy-start.6
  1.7 0.0 copy-start.8
  1.8 7.3 %collective-permute-start.1 = (bf16[64,8,256]{2,1,0:T(8,128)(2,1)S(1)}, bf16[64,8,256]{2,1,0:T(8,128)(2,1)S(1)}, u32[]{:S(2)}, u32[]{:S(2)}) collective-permute-start(bf16[64,8,256]{2,1,0:T(8,128)(2,1)S(1)} %get-tuple-element.38), channel_id=1, source_target_pairs={{8,0},{16,8},{24,16},{32,24},{40,32},{48,40},{56,48},{64,56},{72,6... | collective-permute-start | bytes 786440 | tf_op jit(solution)/shard_map/ppermute | solution.py:554
  9.0 1.9 %collective-permute-start = (bf16[64,8,256]{2,1,0:T(8,128)(2,1)S(1)}, bf16[64,8,256]{2,1,0:T(8,128)(2,1)S(1)}, u32[]{:S(2)}, u32[]{:S(2)}) collective-permute-start(bf16[64,8,256]{2,1,0:T(8,128)(2,1)S(1)} %get-tuple-element.39), channel_id=1, source_target_pairs={{0,8},{8,16},{16,24},{24,32},{32,40},{40,48},{48,56},{56,64},{64,7... | collective-permute-start | bytes 786440 | tf_op jit(solution)/shard_map/ppermute | solution.py:554
  11.0 0.7 convert_element_type.11
  11.7 0.7 subtract_multiply_fusion
  12.3 1.3 %pad_maximum_fusion.2.rows_ref.frame_ref.key_row_ref = f32[8,256]{1,0:T(8,128)} fusion(f32[1,256]{1,0:T(1,128)S(1)} %bitcast.19, f32[1,256]{1,0:T(1,128)S(1)} %bitcast.18, f32[3,256]{1,0:T(4,128)} %param.29, f32[3,256]{1,0:T(4,128)} %param.28), kind=kLoop, calls=%fused_computation.2 | loop fusion | flops 6144 | bytes 16384 | tf_op jit(solution)/shard_map/concatenate | solution.py:602
  13.6 1.8 %pack.1 = bf16[88,384]{1,0:T(8,128)(2,1)} custom-call(bf16[256,384]{1,0:T(8,128)(2,1)} %single_ref.3, f32[8,256]{1,0:T(8,128)} %pad_maximum_fusion.2.rows_ref.frame_ref.key_row_ref), custom_call_target="tpu_custom_call" | custom-call | tf_op jit(solution)/shard_map/pack/pallas_call | solution.py:513
  15.5 4.1 %turn.1 = (bf16[64,64,256]{2,1,0:T(8,128)(2,1)}, bf16[8,64,64]{2,1,0:T(8,128)(2,1)}, bf16[8,64,64]{2,1,0:T(8,128)(2,1)}) custom-call(bf16[64,64,256]{2,1,0:T(8,128)(2,1)} %pair_ref.1), custom_call_target="tpu_custom_call" | custom-call | tf_op jit(solution)/shard_map/turn/pallas_call | solution.py:57
  19.6 5.5 %collective-permute-done.raw_up_ref = bf16[64,8,256]{2,1,0:T(8,128)(2,1)S(1)} collective-permute-done((bf16[64,8,256]{2,1,0:T(8,128)(2,1)S(1)}, bf16[64,8,256]{2,1,0:T(8,128)(2,1)S(1)}, u32[]{:S(2)}, u32[]{:S(2)}) %collective-permute-start) | collective-permute-done | bytes 262176 | tf_op jit(solution)/shard_map/ppermute | solution.py:554
  25.1 0.7 copy-done.3
  25.8 1.9 %rim.1 = (bf16[8,64,256]{2,1,0:T(8,128)(2,1)}, bf16[8,64,256]{2,1,0:T(8,128)(2,1)}, bf16[2,64,64]{2,1,0:T(8,128)(2,1)}, bf16[2,64,64]{2,1,0:T(8,128)(2,1)}) custom-call(bf16[64,8,256]{2,1,0:T(8,128)(2,1)} %copy-done.3, bf16[64,8,256]{2,1,0:T(8,128)(2,1)} %copy-done.2), custom_call_target="tpu_custom_call" | custom-call | tf_op jit(solution)/shard_map/rim/pallas_call | solution.py:88
  27.7 0.8 fusion.2
  28.5 0.9 %pad_maximum_fusion = bf16[10,64,64]{2,1,0:T(8,128)(2,1)S(1)} fusion(bf16[1,64,64]{2,1,0:T(8,128)(2,1)S(1)} %get-tuple-element.44, bf16[8,64,64]{2,1,0:T(8,128)(2,1)} %get-tuple-element.23, bf16[1,64,64]{2,1,0:T(8,128)(2,1)S(1)} %get-tuple-element.45), kind=kLoop, calls=%fused_computation | loop fusion | flops 81920 | bytes 163840 | tf_op jit(solution)/shard_map/concatenate | solution.py:621
  29.4 0.9 %pad_maximum_fusion.1 = bf16[10,64,64]{2,1,0:T(8,128)(2,1)S(1)} fusion(bf16[1,64,64]{2,1,0:T(8,128)(2,1)S(1)} %get-tuple-element.41, bf16[8,64,64]{2,1,0:T(8,128)(2,1)} %get-tuple-element.25, bf16[1,64,64]{2,1,0:T(8,128)(2,1)S(1)} %get-tuple-element.40), kind=kLoop, calls=%fused_computation.1 | loop fusion | flops 81920 | bytes 163840 | tf_op jit(solution)/shard_map/concatenate | solution.py:622
  30.4 1.3 %collective-permute-start.2 = (bf16[10,64,64]{2,1,0:T(8,128)(2,1)S(1)}, bf16[10,64,64]{2,1,0:T(8,128)(2,1)S(1)}, u32[]{:S(2)}, u32[]{:S(2)}) collective-permute-start(bf16[10,64,64]{2,1,0:T(8,128)(2,1)S(1)} %pad_maximum_fusion), channel_id=1, source_target_pairs={{0,1},{1,2},{2,3},{3,4},{4,5},{5,6},{6,7},{8,9},{9,10},{10,11},{11... | collective-permute-start | bytes 245768 | tf_op jit(solution)/shard_map/ppermute | solution.py:554
  31.7 1.3 %collective-permute-start.3 = (bf16[10,64,64]{2,1,0:T(8,128)(2,1)S(1)}, bf16[10,64,64]{2,1,0:T(8,128)(2,1)S(1)}, u32[]{:S(2)}, u32[]{:S(2)}) collective-permute-start(bf16[10,64,64]{2,1,0:T(8,128)(2,1)S(1)} %pad_maximum_fusion.1), channel_id=1, source_target_pairs={{1,0},{2,1},{3,2},{4,3},{5,4},{6,5},{7,6},{9,8},{10,9},{11,10},{12... | collective-permute-start | bytes 245768 | tf_op jit(solution)/shard_map/ppermute | solution.py:554
  33.1 0.6 concatenate.15.params_ref
  33.8 5.0 %keys.1 = (bf16[2,256,512]{2,1,0:T(8,128)(2,1)}, bf16[3,256,512]{2,1,0:T(8,128)(2,1)}, f32[16,256]{1,0:T(8,128)}) custom-call(bf16[256,384]{1,0:T(8,128)(2,1)} %single_ref.3, bf16[192,384]{1,0:T(8,128)(2,1)} %bitcast.14, bf16[192,384]{1,0:T(8,128)(2,1)} %bitcast.15, bf16[432,384]{1,0:T(8,128)(2,1)} %bitcast.12, ...), custom_call_target="tpu_custom_call" | custom-call | tf_op jit(solution)/shard_map/keys/pallas_call | solution.py:355
  38.8 0.6 copy-done.1
  39.4 5.9 %base.1 = (f32[64,16,256]{2,1,0:T(8,128)}, f32[64,16]{1,0:T(8,128)}) custom-call(bf16[88,384]{1,0:T(8,128)(2,1)} %copy-done.1, bf16[192,384]{1,0:T(8,128)(2,1)} %bitcast.16, bf16[144,384]{1,0:T(8,128)(2,1)} %bitcast.17, bf16[3,256,512]{2,1,0:T(8,128)(2,1)} %get-tuple-element.29.key_ref, f32[16,256]{1,0:T(8,128)} %get-tuple-element.30.key_sq_ref, ...), custom_call_target="tpu_custom_call" | custom-call | tf_op jit(solution)/shard_map/base/pallas_call | solution.py:424
  45.3 0.6 copy-done.4
  46.0 0.1 copy-done.5
  46.0 14.3 %main.1 = (bf16[64,64,256]{2,1,0:T(8,128)(2,1)}, f32[64,16,128]{2,1,0:T(8,128)}) custom-call(bf16[8,64,256]{2,1,0:T(8,128)(2,1)} %get-tuple-element.19.up_ref, bf16[64,64,256]{2,1,0:T(8,128)(2,1)} %get-tuple-element.20.own_ref, bf16[8,64,256]{2,1,0:T(8,128)(2,1)} %get-tuple-element.21.down_ref, bf16[10,64,64]{2,1,0:T(8,128)(2,1)} %copy-done.4, ...), custom_call_target="tpu_custom_call" | custom-call | tf_op jit(solution)/shard_map/main/pallas_call | solution.py:268
  60.3 16.6 %all_to_all.10.sums_ref = f32[8,8,16,128]{3,2,1,0:T(8,128)} all-to-all(f32[8,8,16,128]{3,2,1,0:T(8,128)} %bitcast.11), channel_id=1, replica_groups=mesh['row'=32,'col'=8] {'col'}, dimensions={0} | all-to-all | bytes 1048576 | tf_op jit(solution)/shard_map/all_to_all | solution.py:667
  76.9 3.6 %finish.1 = bf16[8,8,384]{2,1,0:T(8,128)(2,1)} custom-call(f32[8,8,16,128]{3,2,1,0:T(8,128)} %all_to_all.10.sums_ref, f32[16,512]{1,0:T(8,128)} %constant.31.clone.owner_ref, f32[64,16]{1,0:T(8,128)} %get-tuple-element.35.frame_ref, bf16[88,384]{1,0:T(8,128)(2,1)} %copy-done.1, bf16[1248,384]{1,0:T(8,128)(2,1)} %w_out_ref.1, f32[8,384]{1,0:T(8,128)} %concatenate.15.params_ref), custom_call_target="tpu_custom_call" | custom-call | tf_op jit(solution)/shard_map/finish/pallas_call | solution.py:491
  80.5 3.3 %all-to-all-start.1 = ((bf16[8,8,384]{2,1,0:T(8,128)(2,1)}), bf16[8,8,384]{2,1,0:T(8,128)(2,1)S(1)}, u32[]{:S(2)}, u32[]{:S(2)}) async-start(bf16[8,8,384]{2,1,0:T(8,128)(2,1)} %finish.1), calls=%async_computation.1 | async-start | bytes 98304 | tf_op jit(solution)/shard_map/all_to_all | solution.py:669
  83.9 2.5 %copy.26 = bf16[64,64,256]{2,1,0:T(8,128)(2,1)} copy(bf16[64,64,256]{2,0,1:T(8,128)(2,1)S(1)} %bitcast.10) | data formatting | bytes 4194304
  86.4 3.7 %all-to-all-done.1 = bf16[8,8,384]{2,1,0:T(8,128)(2,1)S(1)} async-done(((bf16[8,8,384]{2,1,0:T(8,128)(2,1)}), bf16[8,8,384]{2,1,0:T(8,128)(2,1)S(1)}, u32[]{:S(2)}, u32[]{:S(2)}) %all-to-all-start.1) | async-done | bytes 49184 | tf_op jit(solution)/shard_map/all_to_all | solution.py:669
  90.1 0.6 copy.28
  (27 shorter events, 0.1 us)
Async XLA Ops:
  1.7 31.3 %copy-start.9 = (f32[12]{0:T(128)S(1)}, f32[12]{0:T(128)}, u32[]{:S(2)}) copy-start(f32[12]{0:T(128)} %param.38) | copy-start | bytes 148
  1.7 31.3 %copy-start.6 = (f32[384]{0:T(512)S(1)}, f32[384]{0:T(512)}, u32[]{:S(2)}) copy-start(f32[384]{0:T(512)} %param.41) | copy-start | bytes 4612
  1.7 31.3 %copy-start.7 = (f32[64]{0:T(128)S(1)}, f32[64]{0:T(128)}, u32[]{:S(2)}) copy-start(f32[64]{0:T(128)} %param.26) | copy-start | bytes 772
  1.7 31.4 %copy-start.8 = (f32[12]{0:T(128)S(1)}, f32[12]{0:T(128)}, u32[]{:S(2)}) copy-start(f32[12]{0:T(128)} %param.39) | copy-start | bytes 148
  1.8 17.8 %collective-permute-start.1 = (bf16[64,8,256]{2,1,0:T(8,128)(2,1)S(1)}, bf16[64,8,256]{2,1,0:T(8,128)(2,1)S(1)}, u32[]{:S(2)}, u32[]{:S(2)}) collective-permute-start(bf16[64,8,256]{2,1,0:T(8,128)(2,1)S(1)} %get-tuple-element.38), channel_id=1, source_target_pairs={{8,0},{16,8},{24,16},{32,24},{40,32},{48,40},{56,48},{64,56},{72,6... | collective-permute-start | bytes 786440 | tf_op jit(solution)/shard_map/ppermute | solution.py:554
  9.0 16.1 %collective-permute-start = (bf16[64,8,256]{2,1,0:T(8,128)(2,1)S(1)}, bf16[64,8,256]{2,1,0:T(8,128)(2,1)S(1)}, u32[]{:S(2)}, u32[]{:S(2)}) collective-permute-start(bf16[64,8,256]{2,1,0:T(8,128)(2,1)S(1)} %get-tuple-element.39), channel_id=1, source_target_pairs={{0,8},{8,16},{16,24},{24,32},{32,40},{40,48},{48,56},{56,64},{64,7... | collective-permute-start | bytes 786440 | tf_op jit(solution)/shard_map/ppermute | solution.py:554
  15.5 23.3 %collective-permute-start.4 = (bf16[88,384]{1,0:T(8,128)(2,1)}, bf16[88,384]{1,0:T(8,128)(2,1)S(1)}, u32[]{:S(2)}, u32[]{:S(2)}) collective-permute-start(bf16[88,384]{1,0:T(8,128)(2,1)} %pack.1), channel_id=1, source_target_pairs={{0,2},{8,10},{16,18},{24,26},{32,3},{40,11},{48,19},{56,27},{64,0}... | collective-permute-start | bytes 202760 | tf_op jit(solution)/shard_map/ppermute | solution.py:611
  19.6 5.6 %copy-start.2 = (bf16[64,8,256]{2,1,0:T(8,128)(2,1)}, bf16[64,8,256]{2,1,0:T(8,128)(2,1)S(1)}, u32[]{:S(2)}) copy-start(bf16[64,8,256]{2,1,0:T(8,128)(2,1)S(1)} %collective-permute-done.1.raw_down_ref) | copy-start | bytes 786436
  25.1 0.7 copy-start.3
  30.4 14.9 %collective-permute-start.2 = (bf16[10,64,64]{2,1,0:T(8,128)(2,1)S(1)}, bf16[10,64,64]{2,1,0:T(8,128)(2,1)S(1)}, u32[]{:S(2)}, u32[]{:S(2)}) collective-permute-start(bf16[10,64,64]{2,1,0:T(8,128)(2,1)S(1)} %pad_maximum_fusion), channel_id=1, source_target_pairs={{0,1},{1,2},{2,3},{3,4},{4,5},{5,6},{6,7},{8,9},{9,10},{10,11},{11... | collective-permute-start | bytes 245768 | tf_op jit(solution)/shard_map/ppermute | solution.py:554
  31.7 13.6 %collective-permute-start.3 = (bf16[10,64,64]{2,1,0:T(8,128)(2,1)S(1)}, bf16[10,64,64]{2,1,0:T(8,128)(2,1)S(1)}, u32[]{:S(2)}, u32[]{:S(2)}) collective-permute-start(bf16[10,64,64]{2,1,0:T(8,128)(2,1)S(1)} %pad_maximum_fusion.1), channel_id=1, source_target_pairs={{1,0},{2,1},{3,2},{4,3},{5,4},{6,5},{7,6},{9,8},{10,9},{11,10},{12... | collective-permute-start | bytes 245768 | tf_op jit(solution)/shard_map/ppermute | solution.py:554
  38.8 0.6 copy-start.1
  45.3 0.7 copy-start.4
  45.3 0.7 copy-start.5
  60.3 23.6 %copy-start = (bf16[64,64,256]{2,1,0:T(8,128)(2,1)S(1)}, bf16[64,64,256]{2,1,0:T(8,128)(2,1)}, u32[]{:S(2)}) copy-start(bf16[64,64,256]{2,1,0:T(8,128)(2,1)} %get-tuple-element.33) | copy-start | bytes 6291460
  80.5 9.6 %all-to-all-start.1 = ((bf16[8,8,384]{2,1,0:T(8,128)(2,1)}), bf16[8,8,384]{2,1,0:T(8,128)(2,1)S(1)}, u32[]{:S(2)}, u32[]{:S(2)}) async-start(bf16[8,8,384]{2,1,0:T(8,128)(2,1)} %finish.1), calls=%async_computation.1 | async-start | bytes 98304 | tf_op jit(solution)/shard_map/all_to_all | solution.py:669

commit v2 on v1

--- a/solution.py
+++ b/solution.py
@@ -72,22 +72,53 @@
     )(pair)
 
 
-def rim_kernel(raw_up_ref, raw_down_ref, up_ref, down_ref, head_ref, tail_ref):
-    for index, (raw, ref) in enumerate(((raw_up_ref, up_ref), (raw_down_ref, down_ref))):
-        turned = jnp.swapaxes(raw[...], 0, 1)
+def rim_kernel(
+    raw_up_ref,
+    raw_down_ref,
+    own_head_ref,
+    own_tail_ref,
+    up_ref,
+    down_ref,
+    to_left_ref,
+    to_right_ref,
+    near_ref,
+    sems,
+):
+    copies = [
+        pltpu.make_async_copy(raw, near_ref.at[k], sems.at[k])
+        for k, raw in enumerate((raw_up_ref, raw_down_ref))
+    ]
+    for copy in copies:
+        copy.start()
+    inner = own_head_ref.shape[0]
+    to_left_ref[1 : 1 + inner] = own_head_ref[...]
+    to_right_ref[1 : 1 + inner] = own_tail_ref[...]
+    for k, (ref, index) in enumerate(((up_ref, 0), (down_ref, inner + 1))):
+        copies[k].wait()
+        turned = jnp.swapaxes(near_ref[k], 0, 1)
         ref[...] = turned
         head, tail = edge_cells([turned[i] for i in range(8)])
-        head_ref[index] = head
-        tail_ref[index] = tail
-
-
-def rim(raw_up, raw_down):
+        to_left_ref[index] = head
+        to_right_ref[index] = tail
+
+
+def rim(raw_up, raw_down, own_head, own_tail):
     channels, count, cols = raw_up.shape
+    inner = own_head.shape[0]
     rows = jax.ShapeDtypeStruct((count, channels, cols), raw_up.dtype)
-    edge = jax.ShapeDtypeStruct((2, channels, 64), raw_up.dtype)
-    return pl.pallas_call(rim_kernel, out_shape=[rows, rows, edge, edge], name="rim")(
-        raw_up, raw_down
-    )
+    edge = jax.ShapeDtypeStruct((inner + 2, channels, 64), raw_up.dtype)
+    vmem = pl.BlockSpec(memory_space=pltpu.VMEM)
+    return pl.pallas_call(
+        rim_kernel,
+        in_specs=[pl.BlockSpec(memory_space=pl.ANY)] * 2 + [vmem] * 2,
+        out_specs=[vmem] * 4,
+        out_shape=[rows, rows, edge, edge],
+        scratch_shapes=[
+            pltpu.VMEM((2, channels, count, cols), raw_up.dtype),
+            pltpu.SemaphoreType.DMA((2,)),
+        ],
+        name="rim",
+    )(raw_up, raw_down, own_head, own_tail)
 
 
 def as_column(row, count):
@@ -150,16 +181,18 @@
     last = pl.num_programs(0) - 1
     channels = own_ref.shape[1]
     cols = own_ref.shape[2]
-    slot = lax.rem(step, 3)
-
-    def stage(source):
+    slot = lax.rem(step, 4)
+
+    def stage(picked=range(8)):
         lane = lax.broadcasted_iota(jnp.int32, (channels, 128), 1)
         empty = jnp.zeros((channels, 64), jnp.bfloat16)
         before = jnp.concatenate([left_ref[0], empty], axis=1)
         after = jnp.concatenate([right_ref[0], empty], axis=1)
         top = channels
-        for i in range(8):
-            cells = source[i]
+        for i in picked:
+            cells = jnp.where(
+                step == 0, up_ref[i], jnp.where(step == last - 1, down_ref[i], own_ref[i])
+            )
             ahead = [pltpu.roll(cells[:, 128 * k : 128 * k + 128], 8, 1) for k in range(2)]
             fill = pltpu.roll(before, (128 - 8 * i) % 128, 1)
             window_ref[slot, i, 0:top, 0:128] = jnp.where(lane < 8, fill, ahead[0])
@@ -180,27 +213,23 @@
         )
         head_bias_ref[...] = dot32(pick.astype(jnp.bfloat16), raw_bias_ref[...]).astype(jnp.bfloat16)
         shift_ref[...] = jnp.broadcast_to(as_column(params_ref[1:2, :], channels), (channels, cols))
-        stage(up_ref)
-
-    @pl.when(jnp.logical_and(step > 0, step < last))
+
+    @pl.when(step < 3)
     def _():
-        stage(own_ref)
-
-    @pl.when(step == last)
+        stage()
+
+    @pl.when(step >= 3)
     def _():
-        stage(down_ref)
-
-    @pl.when(step >= 2)
-    def _():
-        first = lax.rem(step + 1, 3)
-        middle = lax.rem(step + 2, 3)
+        first = lax.rem(step + 1, 4)
+        middle = lax.rem(step + 2, 4)
+        third = lax.rem(step + 3, 4)
         lane = lax.broadcasted_iota(jnp.int32, (8, 16, 128), 2)
 
         def convolve(i):
             return (
                 jnp.dot(weight_ref[0], window_ref[first, i], preferred_element_type=jnp.float32)
                 + jnp.dot(weight_ref[1], window_ref[middle, i], preferred_element_type=jnp.float32)
-                + jnp.dot(weight_ref[2], window_ref[slot, i], preferred_element_type=jnp.float32)
+                + jnp.dot(weight_ref[2], window_ref[third, i], preferred_element_type=jnp.float32)
             )
 
         shift = shift_ref[...]
@@ -212,6 +241,7 @@
             bent = jnp.where(conv > 0.0, conv, jnp.exp(jnp.minimum(conv, 0.0)) - 1.0)
             cells = window_ref[middle, i, channels : 2 * channels].astype(jnp.float32)
             out_ref[i] = (cells + bent).astype(jnp.bfloat16)
+            stage((i,))
         bias = jnp.stack(
             [
                 jnp.dot(head_bias_ref[...], out_ref[i], preferred_element_type=jnp.float32)
@@ -234,7 +264,7 @@
             ]
         )
         padded = jnp.concatenate([pair_sum, jnp.zeros((8, 16, 64), jnp.float32)], axis=2)
-        row = pl.multiple_of((step - 2) * 8, 8)
+        row = pl.multiple_of((step - 3) * 8, 8)
         sums_ref[pl.ds(row, 8)] = jnp.where(
             lane == 104, peak, jnp.where(lane == 105, total, padded)
         )
@@ -244,6 +274,7 @@
     def _():
         chunk = 256
         sub = lax.broadcasted_iota(jnp.int32, (chunk // 16, 16, 128), 1)
+        lane = lax.broadcasted_iota(jnp.int32, (chunk // 16, 16, 128), 2)
         for part in range(soft_ref.shape[0] // chunk):
             soft = soft_ref[part * chunk : (part + 1) * chunk, :]
             acc = jnp.dot(soft, value_ref[0], preferred_element_type=jnp.float32) + jnp.dot(
@@ -253,27 +284,35 @@
             folded = jnp.sum(acc, axis=1, keepdims=True)
             rows = slice(part * chunk // 16, (part + 1) * chunk // 16)
             kept = sums_ref[rows]
+            marks = jnp.where(
+                lane == 96 + sub,
+                kept[:, :, 104:105],
+                jnp.where(lane == 108 + sub, kept[:, :, 105:106], 0.0),
+            )
+            marks = jnp.sum(jnp.where(sub < 12, marks, 0.0), axis=1, keepdims=True)
             for k in range(4):
                 lanes = folded[:, :, 128 * k : 128 * k + 128]
+                if k == 3:
+                    lanes = lanes + marks
                 kept = jnp.where(sub == 12 + k, lanes, kept)
             sums_ref[rows] = kept
 
 
 def main(up, own, down, left, right, weight, bias, head_bias, base, value, owner):
     row_count, channels, col_count = own.shape
-    steps = row_count // 8 + 2
+    steps = row_count // 8 + 3
     fixed3 = lambda b: (0, 0, 0)
     fixed2 = lambda b: (0, 0)
-    late = lambda b: (jnp.maximum(b - 2, 0), 0, 0)
+    late = lambda b: (jnp.maximum(b - 3, 0), 0, 0)
     return pl.pallas_call(
         main_kernel,
         grid=(steps,),
         in_specs=[
             pl.BlockSpec(up.shape, fixed3),
-            pl.BlockSpec((8, channels, col_count), lambda b: (jnp.clip(b - 1, 0, steps - 3), 0, 0)),
+            pl.BlockSpec((8, channels, col_count), lambda b: (jnp.clip(b - 1, 0, steps - 4), 0, 0)),
             pl.BlockSpec(down.shape, fixed3),
-            pl.BlockSpec((1, channels, 64), lambda b: (b, 0, 0)),
-            pl.BlockSpec((1, channels, 64), lambda b: (b, 0, 0)),
+            pl.BlockSpec((1, channels, 64), lambda b: (jnp.minimum(b, steps - 2), 0, 0)),
+            pl.BlockSpec((1, channels, 64), lambda b: (jnp.minimum(b, steps - 2), 0, 0)),
             pl.BlockSpec(weight.shape, fixed3),
             pl.BlockSpec(bias.shape, fixed2),
             pl.BlockSpec(head_bias.shape, fixed2),
@@ -290,7 +329,7 @@
             jax.ShapeDtypeStruct((row_count, 16, 128), jnp.float32),
         ],
         scratch_shapes=[
-            pltpu.VMEM((3, 8, 3 * channels, col_count), jnp.bfloat16),
+            pltpu.VMEM((4, 8, 3 * channels, col_count), jnp.bfloat16),
             pltpu.VMEM((row_count * 16, col_count), jnp.bfloat16),
             pltpu.VMEM((3, channels, 3 * channels), jnp.bfloat16),
             pltpu.VMEM((16, channels), jnp.bfloat16),
@@ -329,25 +368,32 @@
     rows = single_ref[...]
     key = dot32_nt(rows, w_key_ref[...])
     value = dot32_nt(rows, w_value_ref[...]).astype(jnp.bfloat16)
-    points = to_global(dot32_nt(rows, w_kvpts_ref[...]), frame_columns(frame_ref[...]))
-    point_parts = in_pieces(points, 3)
-    key_parts = in_pieces(
-        jnp.concatenate([key, jnp.zeros((key.shape[0], 256 - key.shape[1]), jnp.float32)], axis=1), 3
-    )
-    whole = jnp.zeros((rows.shape[0], 256), jnp.float32)
+    frame = frame_columns(frame_ref[...])
+    span = w_kvpts_ref.shape[0] // 3
+    local = [dot32_nt(rows, w_kvpts_ref[span * d : span * (d + 1), :]) for d in range(3)]
+    empty = jnp.zeros((key.shape[0], 384 - key.shape[1]), jnp.float32)
+    key_parts = in_pieces(jnp.concatenate([key, empty], axis=1), 3)
+    picked = [jnp.zeros((rows.shape[0], 384), jnp.float32) for _ in range(3)]
+    values = [dot32(value, shift_value_ref[...]), jnp.zeros((rows.shape[0], 512), jnp.float32)]
+    for x in range(3):
+        total = frame[:, 9 + x : 10 + x]
+        for d in range(3):
+            total = total + frame[:, 3 * x + d : 3 * x + d + 1] * local[d]
+        parts = in_pieces(total, 3)
+        own = slice(span * x, span * (x + 1))
+        for index in range(3):
+            picked[index] = picked[index] + dot32(parts[index], pick_key_ref[own, :])
+        for index in range(2):
+            values[index] = values[index] + dot32(parts[index], pick_value_ref[own, :])
     for index in range(3):
-        picked = dot32(point_parts[index], pick_key_ref[...])
-        whole = whole + picked
-        key_ref[index, :, 0:256] = key_parts[index]
-        key_ref[index, :, 256:512] = picked.astype(jnp.bfloat16)
+        key_ref[index] = (key_parts[index].astype(jnp.float32) + picked[index]).astype(jnp.bfloat16)
+    value_ref[0] = values[0].astype(jnp.bfloat16)
+    value_ref[1] = values[1].astype(jnp.bfloat16)
+    whole = picked[0] + picked[1] + picked[2]
     square = jnp.zeros((16, rows.shape[0]), jnp.float32)
     for part in in_pieces(whole * whole, 3):
         square = square + dot32_nt(points_ref[...], part)
     key_sq_ref[...] = square
-    value_ref[0] = (
-        dot32(value, shift_value_ref[...]) + dot32(point_parts[0], pick_value_ref[...])
-    ).astype(jnp.bfloat16)
-    value_ref[1] = dot32(point_parts[1], pick_value_ref[...]).astype(jnp.bfloat16)
 
 
 def keys(single, w_key, w_value, w_kvpts, frame, pick_key, pick_value, shift_value, points):
@@ -356,7 +402,7 @@
         keys_kernel,
         out_shape=[
             jax.ShapeDtypeStruct((2, count, 512), jnp.bfloat16),
-            jax.ShapeDtypeStruct((3, count, 512), jnp.bfloat16),
+            jax.ShapeDtypeStruct((3, count, 384), jnp.bfloat16),
             jax.ShapeDtypeStruct((16, count), jnp.float32),
         ],
         name="keys",
@@ -375,70 +421,77 @@
     base_ref,
     frame_ref,
 ):
-    step = pl.program_id(0)
-    count = base_ref.shape[0]
-
-    @pl.when(step == 0)
-    def _():
-        every = query_ref.shape[0] - 24
-        tail = query_ref[every:, 0:every].astype(jnp.float32)
-        frame_ref[...] = frame_columns(tail[0:8] + tail[8:16] + tail[16:24])
-
-    own = pl.ds(pl.multiple_of(step * count, count), count)
+    every = query_ref.shape[0] - 24
+    tail = query_ref[every:, 0:every].astype(jnp.float32)
+    frames = frame_columns(tail[0:8] + tail[8:16] + tail[16:24])
+    frame_ref[...] = frames
+    joined_keys = jnp.concatenate([key_ref[b] for b in (0, 1, 2, 0, 1, 0)], axis=1)
+    point_scale = as_column(params_ref[2:3, :], 16)
+    chain = as_column(params_ref[3:4, :], 16)
+    shared = 0.5 * point_scale * key_sq_ref[...] + key_row_ref[7:8, :]
+    for chunk in range(every // 16):
+        base_chunk(
+            slice(16 * chunk, 16 * chunk + 16),
+            frames,
+            joined_keys,
+            point_scale,
+            chain,
+            shared,
+            query_ref,
+            w_query_ref,
+            w_qpts_ref,
+            table_ref,
+            key_row_ref,
+            base_ref,
+        )
+
+
+def base_chunk(
+    own,
+    frames,
+    joined_keys,
+    point_scale,
+    chain,
+    shared,
+    query_ref,
+    w_query_ref,
+    w_qpts_ref,
+    table_ref,
+    key_row_ref,
+    base_ref,
+):
+    count = 16
     rows = query_ref[own, :]
-    frame = frame_ref[own, :]
+    frame = frames[own, :]
     query = dot32_nt(rows, w_query_ref[...])
     points = to_global(dot32_nt(rows, w_qpts_ref[...]), frame)
-    points = jnp.concatenate([points, jnp.zeros((count, 256 - points.shape[1]), jnp.float32)], axis=1)
-    query = jnp.concatenate([query, jnp.zeros((count, 256 - query.shape[1]), jnp.float32)], axis=1)
-    point_scale = as_column(params_ref[2:3, :], 16)
-    query = query[:, None, :] * table_ref[:, 0:256][None]
-    scaled = points[:, None, :] * (table_ref[:, 256:512] * point_scale)[None]
-    own_sq = 0.5 * jnp.sum(scaled * points[:, None, :], axis=2, keepdims=True)
-    query_parts = in_pieces(query.reshape(count * 16, 256), 3)
-    point_parts = in_pieces(scaled.reshape(count * 16, 256), 3)
-    total = jnp.zeros((count * 16, key_ref.shape[1]), jnp.float32)
-    for a, b in ((2, 0), (1, 1), (0, 2), (1, 0), (0, 1), (0, 0)):
-        total = total + dot32_nt(
-            jnp.concatenate([query_parts[a], point_parts[a]], axis=1), key_ref[b]
-        )
-    scale = 0.5 * point_scale
-    chain = as_column(params_ref[3:4, :], 16)
+    empty = jnp.zeros((count, 384 - query.shape[1] - points.shape[1]), jnp.float32)
+    lane = lax.broadcasted_iota(jnp.int32, table_ref.shape, 1)
+    table = table_ref[...] * jnp.where(lane < query.shape[1], 1.0, point_scale)
+    features = jnp.concatenate([query, points, empty], axis=1)
+    scaled = features[:, None, :] * table[None]
+    placed = jnp.concatenate([jnp.zeros_like(query), points, empty], axis=1)
+    own_sq = 0.5 * jnp.sum(scaled * placed[:, None, :], axis=2, keepdims=True)
+    joined = in_pieces(scaled.reshape(count * 16, 384), 3)
+    total = dot32_nt(
+        jnp.concatenate([joined[a] for a in (0, 0, 0, 1, 1, 2)], axis=1), joined_keys
+    )
     same = (frame[:, 12:13] == key_row_ref[6:7, :]).astype(jnp.float32)
-    shared = scale * key_sq_ref[...]
-    base_ref[...] = (
-        total.reshape(count, 16, -1)
-        - own_sq
-        - shared[None]
-        + chain[None] * same[:, None, :]
-        - key_row_ref[7:8, :][None]
+    base_ref[own] = (
+        total.reshape(count, 16, -1) - own_sq - shared[None] + chain[None] * same[:, None, :]
     )
 
 
 def base_logits(query, w_query, w_qpts, key, key_sq, table, params, key_row):
     count = query.shape[0] - 24
-    step = 16
-    whole2 = lambda b: (0, 0)
-    whole3 = lambda b: (0, 0, 0)
-    operands = (query, w_query, w_qpts, key, key_sq, table, params, key_row)
     return pl.pallas_call(
         base_kernel,
-        grid=(count // step,),
-        in_specs=[pl.BlockSpec(x.shape, whole3 if x.ndim == 3 else whole2) for x in operands],
-        out_specs=[
-            pl.BlockSpec((step, 16, key.shape[1]), whole3_at),
-            pl.BlockSpec((count, 16), whole2),
-        ],
         out_shape=[
             jax.ShapeDtypeStruct((count, 16, key.shape[1]), jnp.float32),
             jax.ShapeDtypeStruct((count, 16), jnp.float32),
         ],
         name="base",
-    )(*operands)
-
-
-def whole3_at(b):
-    return (b, 0, 0)
+    )(query, w_query, w_qpts, key, key_sq, table, params, key_row)
 
 
 def finish_kernel(
@@ -448,18 +501,37 @@
     parts, count = sums.shape[0], sums.shape[1]
     width = message_ref.shape[1]
     place = lax.axis_index("col") * count
-    live = lax.broadcasted_iota(jnp.int32, sums.shape[:3] + (1,), 2) < 12
-    peaks = jnp.where(live, sums[:, :, :, 104:105], 0.0)
-    scales = jnp.exp(peaks - jnp.max(peaks, axis=0, keepdims=True))
-    counts = jnp.where(live, sums[:, :, :, 105:106], 1.0)
-    totals = jnp.sum(counts * scales, axis=0, keepdims=True)
-    scales = scales / totals
-    means = jnp.sum(sums * scales, axis=0)
-    flats = []
-    for k in range(4):
-        own = owner_ref[:, 128 * k : 128 * k + 128]
-        lanes = jnp.sum(scales * own[None, None], axis=2)
-        flats.append(jnp.sum(sums[:, :, 12 + k, :] * lanes, axis=0))
+    marks = sums[:, :, 15, :]
+    lane = lax.broadcasted_iota(jnp.int32, (1, 1, 128), 2)
+    live = jnp.logical_and(lane >= 96, lane < 108)
+    grown = jnp.exp(marks - jnp.max(marks, axis=0, keepdims=True))
+    moved = pltpu.roll(grown.reshape(parts * count, 128), 12, 1).reshape(parts, count, 128)
+    totals = pltpu.roll(jnp.sum(marks * moved, axis=0), 116, 1)[None]
+    scales = jnp.where(live, grown / jnp.where(live, totals, 1.0), 0.0)
+    turned = 96 + lax.broadcasted_iota(jnp.int32, (16, 128), 0) == lax.broadcasted_iota(
+        jnp.int32, (16, 128), 1
+    )
+    columns = jnp.sum(
+        jnp.where(turned[None, None], scales[:, :, None, :], 0.0), axis=3, keepdims=True
+    )
+    means = jnp.sum(sums * columns, axis=0)
+    rows = scales.reshape(parts * count, 128)
+    owner = jnp.concatenate(
+        [
+            jnp.zeros((96, owner_ref.shape[1]), jnp.float32),
+            owner_ref[...],
+            jnp.zeros((16, owner_ref.shape[1]), jnp.float32),
+        ],
+        axis=0,
+    ).astype(jnp.bfloat16)
+    lanes = jnp.zeros((parts * count, owner_ref.shape[1]), jnp.float32)
+    for part in reversed(in_pieces(rows, 3)):
+        lanes = lanes + dot32(part, owner)
+    lanes = lanes.reshape(parts, count, -1)
+    flats = [
+        jnp.sum(sums[:, :, 12 + k, :] * lanes[:, :, 128 * k : 128 * k + 128], axis=0)
+        for k in range(4)
+    ]
     flat = jnp.concatenate(flats, axis=1)
     frame = frame_ref[pl.ds(pl.multiple_of(place, count), count), :]
     centred = [flat[:, 192 + 96 * x : 288 + 96 * x] - frame[:, 9 + x : 10 + x] for x in range(3)]
@@ -495,11 +567,15 @@
     )(sums, owner, frame, message, w_out, params)
 
 
-def pack_kernel(single_ref, rows_ref, message_ref):
+def pack_kernel(single_ref, quat_ref, trans_ref, chain_ref, mask_ref, message_ref, rows_ref):
     count = message_ref.shape[0] - 24
     width = message_ref.shape[1]
     slots = single_ref.shape[0] // count
     slot = lax.axis_index("row") % slots
+    rows_ref[0:3, :] = quat_ref[...]
+    rows_ref[3:6, :] = trans_ref[...]
+    rows_ref[6:7, :] = chain_ref[...].astype(jnp.float32)[None, :]
+    rows_ref[7:8, :] = mask_penalty * (1.0 - mask_ref[...].astype(jnp.float32)[None, :])
     message_ref[0:count, :] = single_ref[pl.ds(pl.multiple_of(slot * count, count), count), :]
     rows = rows_ref[:, 0:count]
     for k in range(1, slots):
@@ -509,22 +585,25 @@
         message_ref[count + 8 * k : count + 8 * k + 8, :] = part
 
 
-def pack(single, rows, count):
+def pack(single, quat_vec, trans, chain_id, residue_mask, count):
     return pl.pallas_call(
         pack_kernel,
-        out_shape=jax.ShapeDtypeStruct((count + 24, single.shape[1]), single.dtype),
+        out_shape=[
+            jax.ShapeDtypeStruct((count + 24, single.shape[1]), single.dtype),
+            jax.ShapeDtypeStruct((8, single.shape[0]), jnp.float32),
+        ],
         name="pack",
-    )(single, rows)
+    )(single, quat_vec, trans, chain_id, residue_mask)
 
 
 def tables(head_count, head_dim, query_points, value_points):
     both = query_points + value_points
     span = 3 * head_count * both
-    pick_key = np.zeros((span, 256), np.float32)
+    pick_key = np.zeros((span, 384), np.float32)
     pick_value = np.zeros((span, 512), np.float32)
     shift_value = np.zeros((head_count * head_dim, 512), np.float32)
-    points = np.zeros((16, 256), np.float32)
-    scalars = np.zeros((16, 256), np.float32)
+    points = np.zeros((16, 384), np.float32)
+    scalars = np.zeros((16, 384), np.float32)
     owner = np.zeros((16, 512), np.float32)
     for h in range(head_count):
         for d in range(head_dim):
@@ -535,7 +614,7 @@
         for x in range(3):
             first = (x * head_count + h) * both
             for p in range(query_points):
-                lane = (x * head_count + h) * query_points + p
+                lane = head_count * head_dim + (x * head_count + h) * query_points + p
                 pick_key[first + p, lane] = 1.0
                 points[h, lane] = 1.0
             for p in range(value_points):
@@ -599,16 +678,8 @@
     raw_up = shifted(pair[:, row_count - DILATION_STEP :], "row", True)
     raw_down = shifted(pair[:, :DILATION_STEP], "row", False)
     routes = query_routes(n_row, n_col)
-    rows = jnp.concatenate(
-        [
-            quat_vec,
-            trans,
-            chain_id.astype(jnp.float32)[None, :],
-            mask_penalty * (1.0 - residue_mask.astype(jnp.float32))[None, :],
-        ],
-        axis=0,
-    )
-    message = lax.ppermute(pack(single, rows, row_count), ("row", "col"), routes)
+    message, rows = pack(single, quat_vec, trans, chain_id, residue_mask, row_count)
+    message = lax.ppermute(message, ("row", "col"), routes)
     point_scale = logit_scale * jax.nn.softplus(head_weight) * math.sqrt(2.0 / (9.0 * query_points))
     wide = lambda row: jnp.pad(row, (0, width - row.shape[0]))[None, :]
     params = jnp.concatenate(
@@ -617,12 +688,6 @@
         axis=0,
     )
     own, own_head, own_tail = turn(pair)
-    up, down, rim_head, rim_tail = rim(raw_up, raw_down)
-    to_right = jnp.concatenate([rim_tail[:1], own_tail, rim_tail[1:]], axis=0)
-    to_left = jnp.concatenate([rim_head[:1], own_head, rim_head[1:]], axis=0)
-    to_right, to_left, key_rows = lax.optimization_barrier((to_right, to_left, rows))
-    left = shifted(to_right, "col", True)
-    right = shifted(to_left, "col", False)
     pick_key, pick_value, shift_value, points, scalars, owner = tables(
         head_count, head_dim, query_points, value_points
     )
@@ -631,13 +696,18 @@
         w_key.T,
         w_value.T,
         w_kvpts.T,
-        key_rows,
+        rows,
         jnp.asarray(pick_key, jnp.bfloat16),
         jnp.asarray(pick_value, jnp.bfloat16),
         jnp.asarray(shift_value, jnp.bfloat16),
         jnp.asarray(points, jnp.bfloat16),
     )
-    table = np.concatenate([scalars * (logit_scale / math.sqrt(head_dim)), points], axis=1)
+    raw_up, raw_down, key_sq = lax.optimization_barrier((raw_up, raw_down, key_sq))
+    up, down, to_left, to_right = rim(raw_up, raw_down, own_head, own_tail)
+    to_right, to_left, key_rows = lax.optimization_barrier((to_right, to_left, rows))
+    left = shifted(to_right, "col", True)
+    right = shifted(to_left, "col", False)
+    table = scalars * (logit_scale / math.sqrt(head_dim)) + points
     base, frame = base_logits(
         message,
         w_query.T,

time: 92.4 us -> 85.1 us (0.921)
  other arithmetic: 4.58 us -> 0.01 us
  Pallas kernels: 36.6 us -> 35.3 us
    concatenate x3 -> x0, other arithmetic: 3.2 us -> none  [the longest x1 1.31 us: per_device(): jnp.concatenate([quat_vec, trans, chain_id.astype(jnp.float32)[None, :],...]
    pallas_call x1, Pallas kernels: 14.3 us -> 13.2 us  [main(): pl.pallas_call(main_kernel, grid=(steps,), in_specs=[pl.BlockSpec(up.shap...]
  transfers between devices with their start and end apart: 6 -> 6, of which waited for: 2 -> 3; matrix products, arithmetic and copies ran while one was open for 9% -> 4% of each run, Pallas kernels for 21% -> 23%
where the time goes in v2:
time: 85.1 us; the launch traced here: 83.5 us
  Pallas kernels  35.3 us (41%)
  blocking collectives  16.4 us (19%)
  starting transfers between devices  15.1 us (18%)
  waiting for transfers between devices  8.9 us (10%)
  local copies, waits for them, and re-layouts  6.84 us (8%)
    all_to_all x1, blocking collectives, per_device(): sums = lax.all_to_all(sums, 'col', 0, 0, tiled=False)  16.4 us
    pallas_call x1, Pallas kernels, main(): pl.pallas_call(main_kernel, grid=(steps,), in_specs=[pl.BlockSpec(up.shap...  13.2 us
    ppermute x4, starting transfers between devices, shifted(): return lax.ppermute(cells, axis, routes)  11.7 us
    pallas_call x1, Pallas kernels, base_logits(): pl.pallas_call(base_kernel, out_shape=[jax.ShapeDtypeStruct((count, 16, k...  5.35 us
    ppermute x4, waiting for transfers between devices, shifted(): return lax.ppermute(cells, axis, routes)  5.19 us
    unnamed x22, local copies, waits for them, and re-layouts  5.12 us
    pallas_call x1, Pallas kernels, keys(): pl.pallas_call(keys_kernel, out_shape=[jax.ShapeDtypeStruct((2, count, 51...  4.47 us
    pallas_call x1, Pallas kernels, turn(): pl.pallas_call(turn_kernel, grid=(row_count // step,), in_specs=[pl.Block...  4.08 us
  transfers between devices with their start and end apart: 6, of which 3 were waited for; matrix products, arithmetic and copies ran while one was open for 4% of the time, Pallas kernels for 23%

profile of v2, /device:TPU:4, one launch (start us, length us, event | category | flops | bytes accessed | tf_op | source)
XLA Modules:
  0.0 83.5 jit_solution(14848025156138644513)
XLA Ops:
  0.6 1.1 %fusion.1 = (bf16[64,8,256]{2,1,0:T(8,128)(2,1)S(1)}, bf16[64,8,256]{2,1,0:T(8,128)(2,1)S(1)}) fusion(bf16[64,64,256]{2,1,0:T(8,128)(2,1)} %pair_ref.1), kind=kLoop, calls=%fused_computation.2 | loop fusion | bytes 1048576 | tf_op jit(solution)/shard_map/slice | solution.py:679
  1.7 7.1 %collective-permute-start.1 = (bf16[64,8,256]{2,1,0:T(8,128)(2,1)S(1)}, bf16[64,8,256]{2,1,0:T(8,128)(2,1)S(1)}, u32[]{:S(2)}, u32[]{:S(2)}) collective-permute-start(bf16[64,8,256]{2,1,0:T(8,128)(2,1)S(1)} %get-tuple-element.48), channel_id=1, source_target_pairs={{8,0},{16,8},{24,16},{32,24},{40,32},{48,40},{56,48},{64,56},{72,6... | collective-permute-start | bytes 786440 | tf_op jit(solution)/shard_map/ppermute | solution.py:633
  8.9 1.9 %collective-permute-start = (bf16[64,8,256]{2,1,0:T(8,128)(2,1)S(1)}, bf16[64,8,256]{2,1,0:T(8,128)(2,1)S(1)}, u32[]{:S(2)}, u32[]{:S(2)}) collective-permute-start(bf16[64,8,256]{2,1,0:T(8,128)(2,1)S(1)} %get-tuple-element.49), channel_id=1, source_target_pairs={{0,8},{8,16},{16,24},{24,32},{32,40},{40,48},{48,56},{56,64},{64,7... | collective-permute-start | bytes 786440 | tf_op jit(solution)/shard_map/ppermute | solution.py:633
  10.8 1.9 %pack.1 = (bf16[88,384]{1,0:T(8,128)(2,1)}, f32[8,256]{1,0:T(8,128)}) custom-call(bf16[256,384]{1,0:T(8,128)(2,1)} %single_ref.3, f32[3,256]{1,0:T(4,128)} %quat_ref.1, f32[3,256]{1,0:T(4,128)} %trans_ref.1, s32[256]{0:T(256)} %chain_ref.1, s32[256]{0:T(256)} %mask_ref.1), custom_call_target="tpu_custom_call" | custom-call | tf_op jit(solution)/shard_map/pack/pallas_call | solution.py:589
  12.7 0.0 copy-start.8
  12.7 0.1 collective-permute-start.4
  12.8 4.1 %turn.1 = (bf16[64,64,256]{2,1,0:T(8,128)(2,1)}, bf16[8,64,64]{2,1,0:T(8,128)(2,1)}, bf16[8,64,64]{2,1,0:T(8,128)(2,1)}) custom-call(bf16[64,64,256]{2,1,0:T(8,128)(2,1)} %pair_ref.1), custom_call_target="tpu_custom_call" | custom-call | tf_op jit(solution)/shard_map/turn/pallas_call | solution.py:57
  16.9 4.5 %keys.1 = (bf16[2,256,512]{2,1,0:T(8,128)(2,1)}, bf16[3,256,384]{2,1,0:T(8,128)(2,1)}, f32[16,256]{1,0:T(8,128)}) custom-call(bf16[256,384]{1,0:T(8,128)(2,1)} %single_ref.3, bf16[192,384]{1,0:T(8,128)(2,1)} %bitcast.12, bf16[192,384]{1,0:T(8,128)(2,1)} %bitcast.13, bf16[432,384]{1,0:T(8,128)(2,1)} %bitcast.10, ...), custom_call_target="tpu_custom_call" | custom-call | tf_op jit(solution)/shard_map/keys/pallas_call | solution.py:401
  21.3 0.0 collective-permute-done.1.raw_down_ref
  21.3 3.2 %collective-permute-done.raw_up_ref = bf16[64,8,256]{2,1,0:T(8,128)(2,1)S(1)} collective-permute-done((bf16[64,8,256]{2,1,0:T(8,128)(2,1)S(1)}, bf16[64,8,256]{2,1,0:T(8,128)(2,1)S(1)}, u32[]{:S(2)}, u32[]{:S(2)}) %collective-permute-start) | collective-permute-done | bytes 262176 | tf_op jit(solution)/shard_map/ppermute | solution.py:633
  24.6 0.0 copy-done.2
  24.6 0.7 copy-done.3
  25.3 3.0 %rim.1 = (bf16[8,64,256]{2,1,0:T(8,128)(2,1)}, bf16[8,64,256]{2,1,0:T(8,128)(2,1)}, bf16[10,64,64]{2,1,0:T(8,128)(2,1)}, bf16[10,64,64]{2,1,0:T(8,128)(2,1)}) custom-call(bf16[64,8,256]{2,1,0:T(8,128)(2,1)} %copy-done.3, bf16[64,8,256]{2,1,0:T(8,128)(2,1)} %copy-done.2, bf16[8,64,64]{2,1,0:T(8,128)(2,1)} %get-tuple-element.28.own_head_ref, ...), custom_call_target="tpu_custom_call" | custom-call | tf_op jit(solution)/shard_map/rim/pallas_call | solution.py:111
  28.3 1.3 %collective-permute-start.2 = (bf16[10,64,64]{2,1,0:T(8,128)(2,1)}, bf16[10,64,64]{2,1,0:T(8,128)(2,1)S(1)}, u32[]{:S(2)}, u32[]{:S(2)}) collective-permute-start(bf16[10,64,64]{2,1,0:T(8,128)(2,1)} %get-tuple-element.35), channel_id=1, source_target_pairs={{0,1},{1,2},{2,3},{3,4},{4,5},{5,6},{6,7},{8,9},{9,10},{10,11},{11... | collective-permute-start | bytes 245768 | tf_op jit(solution)/shard_map/ppermute | solution.py:633
  29.6 1.3 %collective-permute-start.3 = (bf16[10,64,64]{2,1,0:T(8,128)(2,1)}, bf16[10,64,64]{2,1,0:T(8,128)(2,1)S(1)}, u32[]{:S(2)}, u32[]{:S(2)}) collective-permute-start(bf16[10,64,64]{2,1,0:T(8,128)(2,1)} %get-tuple-element.36), channel_id=1, source_target_pairs={{1,0},{2,1},{3,2},{4,3},{5,4},{6,5},{7,6},{9,8},{10,9},{11,10},{12... | collective-permute-start | bytes 245768 | tf_op jit(solution)/shard_map/ppermute | solution.py:633
  30.9 0.0 copy-done.9
  31.0 0.6 concatenate.3.params_ref
  31.7 0.0 collective-permute-done.4.query_ref.message_ref
  31.7 0.6 copy-done.1
  32.3 5.4 %base.1 = (f32[64,16,256]{2,1,0:T(8,128)}, f32[64,16]{1,0:T(8,128)}) custom-call(bf16[88,384]{1,0:T(8,128)(2,1)} %copy-done.1, bf16[192,384]{1,0:T(8,128)(2,1)} %bitcast.14, bf16[144,384]{1,0:T(8,128)(2,1)} %bitcast.15, bf16[3,256,384]{2,1,0:T(8,128)(2,1)} %get-tuple-element.38.key_ref, f32[16,256]{1,0:T(8,128)} %get-tuple-element.39.key_sq_ref, ...), custom_call_target="tpu_custom_call" | custom-call | tf_op jit(solution)/shard_map/base/pallas_call | solution.py:487
  37.7 0.0 collective-permute-done.2.left_ref
  37.7 1.9 %collective-permute-done.3.right_ref = bf16[10,64,64]{2,1,0:T(8,128)(2,1)S(1)} collective-permute-done((bf16[10,64,64]{2,1,0:T(8,128)(2,1)}, bf16[10,64,64]{2,1,0:T(8,128)(2,1)S(1)}, u32[]{:S(2)}, u32[]{:S(2)}) %collective-permute-start.3) | collective-permute-done | bytes 81952 | tf_op jit(solution)/shard_map/ppermute | solution.py:633
  39.6 0.0 copy-done.4
  39.6 0.6 copy-done.5
  40.3 13.2 %main.1 = (bf16[64,64,256]{2,1,0:T(8,128)(2,1)}, f32[64,16,128]{2,1,0:T(8,128)}) custom-call(bf16[8,64,256]{2,1,0:T(8,128)(2,1)} %get-tuple-element.30.up_ref, bf16[64,64,256]{2,1,0:T(8,128)(2,1)} %get-tuple-element.31.own_ref, bf16[8,64,256]{2,1,0:T(8,128)(2,1)} %get-tuple-element.32.down_ref, bf16[10,64,64]{2,1,0:T(8,128)(2,1)} %copy-done.4, ...), custom_call_target="tpu_custom_call" | custom-call | tf_op jit(solution)/shard_map/main/pallas_call | solution.py:307
  53.5 0.0 copy-start
  53.5 16.4 %all_to_all.10.sums_ref = f32[8,8,16,128]{3,2,1,0:T(8,128)} all-to-all(f32[8,8,16,128]{3,2,1,0:T(8,128)} %bitcast.9), channel_id=1, replica_groups=mesh['row'=32,'col'=8] {'col'}, dimensions={0} | all-to-all | bytes 1048576 | tf_op jit(solution)/shard_map/all_to_all | solution.py:737
  69.9 3.3 %finish.1 = bf16[8,8,384]{2,1,0:T(8,128)(2,1)} custom-call(f32[8,8,16,128]{3,2,1,0:T(8,128)} %all_to_all.10.sums_ref, f32[16,512]{1,0:T(8,128)} %constant.27.clone.owner_ref, f32[64,16]{1,0:T(8,128)} %get-tuple-element.45.frame_ref, bf16[88,384]{1,0:T(8,128)(2,1)} %copy-done.1, bf16[1248,384]{1,0:T(8,128)(2,1)} %w_out_ref.1, f32[8,384]{1,0:T(8,128)} %concatenate.3.params_ref), custom_call_target="tpu_custom_call" | custom-call | tf_op jit(solution)/shard_map/finish/pallas_call | solution.py:563
  73.2 3.3 %all-to-all-start.1 = ((bf16[8,8,384]{2,1,0:T(8,128)(2,1)}), bf16[8,8,384]{2,1,0:T(8,128)(2,1)S(1)}, u32[]{:S(2)}, u32[]{:S(2)}) async-start(bf16[8,8,384]{2,1,0:T(8,128)(2,1)} %finish.1), calls=%async_computation.1 | async-start | bytes 98304 | tf_op jit(solution)/shard_map/all_to_all | solution.py:739
  76.6 2.5 %copy.26 = bf16[64,64,256]{2,1,0:T(8,128)(2,1)} copy(bf16[64,64,256]{2,0,1:T(8,128)(2,1)S(1)} %bitcast.8) | data formatting | bytes 4194304
  79.1 3.7 %all-to-all-done.1 = bf16[8,8,384]{2,1,0:T(8,128)(2,1)S(1)} async-done(((bf16[8,8,384]{2,1,0:T(8,128)(2,1)}), bf16[8,8,384]{2,1,0:T(8,128)(2,1)S(1)}, u32[]{:S(2)}, u32[]{:S(2)}) %all-to-all-start.1) | async-done | bytes 49184 | tf_op jit(solution)/shard_map/all_to_all | solution.py:739
  82.8 0.6 copy.28
  (21 shorter events, 0.1 us)
Async XLA Ops:
  1.7 19.6 %collective-permute-start.1 = (bf16[64,8,256]{2,1,0:T(8,128)(2,1)S(1)}, bf16[64,8,256]{2,1,0:T(8,128)(2,1)S(1)}, u32[]{:S(2)}, u32[]{:S(2)}) collective-permute-start(bf16[64,8,256]{2,1,0:T(8,128)(2,1)S(1)} %get-tuple-element.48), channel_id=1, source_target_pairs={{8,0},{16,8},{24,16},{32,24},{40,32},{48,40},{56,48},{64,56},{72,6... | collective-permute-start | bytes 786440 | tf_op jit(solution)/shard_map/ppermute | solution.py:633
  8.9 15.7 %collective-permute-start = (bf16[64,8,256]{2,1,0:T(8,128)(2,1)S(1)}, bf16[64,8,256]{2,1,0:T(8,128)(2,1)S(1)}, u32[]{:S(2)}, u32[]{:S(2)}) collective-permute-start(bf16[64,8,256]{2,1,0:T(8,128)(2,1)S(1)} %get-tuple-element.49), channel_id=1, source_target_pairs={{0,8},{8,16},{16,24},{24,32},{32,40},{40,48},{48,56},{56,64},{64,7... | collective-permute-start | bytes 786440 | tf_op jit(solution)/shard_map/ppermute | solution.py:633
  12.7 18.2 %copy-start.9 = (f32[12]{0:T(128)S(1)}, f32[12]{0:T(128)}, u32[]{:S(2)}) copy-start(f32[12]{0:T(128)} %param.38) | copy-start | bytes 148
  12.7 18.3 %copy-start.6 = (f32[384]{0:T(512)S(1)}, f32[384]{0:T(512)}, u32[]{:S(2)}) copy-start(f32[384]{0:T(512)} %param.41) | copy-start | bytes 4612
  12.7 18.3 %copy-start.7 = (f32[64]{0:T(128)S(1)}, f32[64]{0:T(128)}, u32[]{:S(2)}) copy-start(f32[64]{0:T(128)} %param.26) | copy-start | bytes 772
  12.7 18.3 %copy-start.8 = (f32[12]{0:T(128)S(1)}, f32[12]{0:T(128)}, u32[]{:S(2)}) copy-start(f32[12]{0:T(128)} %param.39) | copy-start | bytes 148
  12.7 19.0 %collective-permute-start.4 = (bf16[88,384]{1,0:T(8,128)(2,1)}, bf16[88,384]{1,0:T(8,128)(2,1)S(1)}, u32[]{:S(2)}, u32[]{:S(2)}) collective-permute-start(bf16[88,384]{1,0:T(8,128)(2,1)} %get-tuple-element.37), channel_id=1, source_target_pairs={{0,2},{8,10},{16,18},{24,26},{32,3},{40,11},{48,19},{56,27},{64,0}... | collective-permute-start | bytes 202760 | tf_op jit(solution)/shard_map/ppermute | solution.py:682
  21.3 3.2 %copy-start.2 = (bf16[64,8,256]{2,1,0:T(8,128)(2,1)}, bf16[64,8,256]{2,1,0:T(8,128)(2,1)S(1)}, u32[]{:S(2)}) copy-start(bf16[64,8,256]{2,1,0:T(8,128)(2,1)S(1)} %collective-permute-done.1.raw_down_ref) | copy-start | bytes 786436
  24.6 0.7 copy-start.3
  28.3 9.4 %collective-permute-start.2 = (bf16[10,64,64]{2,1,0:T(8,128)(2,1)}, bf16[10,64,64]{2,1,0:T(8,128)(2,1)S(1)}, u32[]{:S(2)}, u32[]{:S(2)}) collective-permute-start(bf16[10,64,64]{2,1,0:T(8,128)(2,1)} %get-tuple-element.35), channel_id=1, source_target_pairs={{0,1},{1,2},{2,3},{3,4},{4,5},{5,6},{6,7},{8,9},{9,10},{10,11},{11... | collective-permute-start | bytes 245768 | tf_op jit(solution)/shard_map/ppermute | solution.py:633
  29.6 10.0 %collective-permute-start.3 = (bf16[10,64,64]{2,1,0:T(8,128)(2,1)}, bf16[10,64,64]{2,1,0:T(8,128)(2,1)S(1)}, u32[]{:S(2)}, u32[]{:S(2)}) collective-permute-start(bf16[10,64,64]{2,1,0:T(8,128)(2,1)} %get-tuple-element.36), channel_id=1, source_target_pairs={{1,0},{2,1},{3,2},{4,3},{5,4},{6,5},{7,6},{9,8},{10,9},{11,10},{12... | collective-permute-start | bytes 245768 | tf_op jit(solution)/shard_map/ppermute | solution.py:633
  31.7 0.6 copy-start.1
  37.7 2.0 %copy-start.4 = (bf16[10,64,64]{2,1,0:T(8,128)(2,1)}, bf16[10,64,64]{2,1,0:T(8,128)(2,1)S(1)}, u32[]{:S(2)}) copy-start(bf16[10,64,64]{2,1,0:T(8,128)(2,1)S(1)} %collective-permute-done.2.left_ref) | copy-start | bytes 245764
  39.6 0.7 copy-start.5
  53.5 23.1 %copy-start = (bf16[64,64,256]{2,1,0:T(8,128)(2,1)S(1)}, bf16[64,64,256]{2,1,0:T(8,128)(2,1)}, u32[]{:S(2)}) copy-start(bf16[64,64,256]{2,1,0:T(8,128)(2,1)} %get-tuple-element.43) | copy-start | bytes 6291460
  73.2 9.6 %all-to-all-start.1 = ((bf16[8,8,384]{2,1,0:T(8,128)(2,1)}), bf16[8,8,384]{2,1,0:T(8,128)(2,1)S(1)}, u32[]{:S(2)}, u32[]{:S(2)}) async-start(bf16[8,8,384]{2,1,0:T(8,128)(2,1)} %finish.1), calls=%async_computation.1 | async-start | bytes 98304 | tf_op jit(solution)/shard_map/all_to_all | solution.py:739

commit v3 on v2

--- a/solution.py
+++ b/solution.py
@@ -359,7 +359,6 @@
     frame_ref,
     pick_key_ref,
     pick_value_ref,
-    shift_value_ref,
     points_ref,
     value_ref,
     key_ref,
@@ -373,8 +372,10 @@
     local = [dot32_nt(rows, w_kvpts_ref[span * d : span * (d + 1), :]) for d in range(3)]
     empty = jnp.zeros((key.shape[0], 384 - key.shape[1]), jnp.float32)
     key_parts = in_pieces(jnp.concatenate([key, empty], axis=1), 3)
-    picked = [jnp.zeros((rows.shape[0], 384), jnp.float32) for _ in range(3)]
-    values = [dot32(value, shift_value_ref[...]), jnp.zeros((rows.shape[0], 512), jnp.float32)]
+    empty = jnp.zeros((key.shape[0], 512 - value.shape[1]), jnp.float32)
+    whole_value = jnp.concatenate([value.astype(jnp.float32), empty], axis=1)
+    picked = [jnp.zeros((rows.shape[0], 256), jnp.float32) for _ in range(3)]
+    values = [whole_value, jnp.zeros((rows.shape[0], 512), jnp.float32)]
     for x in range(3):
         total = frame[:, 9 + x : 10 + x]
         for d in range(3):
@@ -386,7 +387,11 @@
         for index in range(2):
             values[index] = values[index] + dot32(parts[index], pick_value_ref[own, :])
     for index in range(3):
-        key_ref[index] = (key_parts[index].astype(jnp.float32) + picked[index]).astype(jnp.bfloat16)
+        part = key_parts[index]
+        key_ref[index, :, 0:128] = part[:, 0:128]
+        key_ref[index, :, 128:384] = (part[:, 128:384].astype(jnp.float32) + picked[index]).astype(
+            jnp.bfloat16
+        )
     value_ref[0] = values[0].astype(jnp.bfloat16)
     value_ref[1] = values[1].astype(jnp.bfloat16)
     whole = picked[0] + picked[1] + picked[2]
@@ -396,7 +401,7 @@
     key_sq_ref[...] = square
 
 
-def keys(single, w_key, w_value, w_kvpts, frame, pick_key, pick_value, shift_value, points):
+def keys(single, w_key, w_value, w_kvpts, frame, pick_key, pick_value, points):
     count = single.shape[0]
     return pl.pallas_call(
         keys_kernel,
@@ -406,7 +411,7 @@
             jax.ShapeDtypeStruct((16, count), jnp.float32),
         ],
         name="keys",
-    )(single, w_key, w_value, w_kvpts, frame, pick_key, pick_value, shift_value, points)
+    )(single, w_key, w_value, w_kvpts, frame, pick_key, pick_value, points)
 
 
 def base_kernel(
@@ -601,7 +606,6 @@
     span = 3 * head_count * both
     pick_key = np.zeros((span, 384), np.float32)
     pick_value = np.zeros((span, 512), np.float32)
-    shift_value = np.zeros((head_count * head_dim, 512), np.float32)
     points = np.zeros((16, 384), np.float32)
     scalars = np.zeros((16, 384), np.float32)
     owner = np.zeros((16, 512), np.float32)
@@ -610,7 +614,6 @@
             lane = h * head_dim + d
             scalars[h, lane] = 1.0
             owner[h, lane] = 1.0
-            shift_value[lane, lane] = 1.0
         for x in range(3):
             first = (x * head_count + h) * both
             for p in range(query_points):
@@ -621,7 +624,7 @@
                 lane = head_count * head_dim + (x * head_count + h) * value_points + p
                 pick_value[first + query_points + p, lane] = 1.0
                 owner[h, lane] = 1.0
-    return pick_key, pick_value, shift_value, points, scalars, owner
+    return pick_key, pick_value, points, scalars, owner
 
 
 def shifted(cells, axis, forward):
@@ -688,7 +691,7 @@
         axis=0,
     )
     own, own_head, own_tail = turn(pair)
-    pick_key, pick_value, shift_value, points, scalars, owner = tables(
+    pick_key, pick_value, points, scalars, owner = tables(
         head_count, head_dim, query_points, value_points
     )
     value, key, key_sq = keys(
@@ -697,10 +700,9 @@
         w_value.T,
         w_kvpts.T,
         rows,
-        jnp.asarray(pick_key, jnp.bfloat16),
+        jnp.asarray(pick_key[:, 128:], jnp.bfloat16),
         jnp.asarray(pick_value, jnp.bfloat16),
-        jnp.asarray(shift_value, jnp.bfloat16),
-        jnp.asarray(points, jnp.bfloat16),
+        jnp.asarray(points[:, 128:], jnp.bfloat16),
     )
     raw_up, raw_down, key_sq = lax.optimization_barrier((raw_up, raw_down, key_sq))
     up, down, to_left, to_right = rim(raw_up, raw_down, own_head, own_tail)

time: 85.1 us -> 84.6 us (level)
  transfers between devices with their start and end apart: 6 -> 6, of which waited for: 3 -> 3; matrix products, arithmetic and copies ran while one was open for 4% -> 4% of each run, Pallas kernels for 23% -> 22%
where the time goes in v3:
time: 84.6 us; the launch traced here: 83 us
  Pallas kernels  34.8 us (41%)
  blocking collectives  16.4 us (19%)
  starting transfers between devices  15.1 us (18%)
  waiting for transfers between devices  8.92 us (11%)
  local copies, waits for them, and re-layouts  6.82 us (8%)
    all_to_all x1, blocking collectives, per_device(): sums = lax.all_to_all(sums, 'col', 0, 0, tiled=False)  16.4 us
    pallas_call x1, Pallas kernels, main(): pl.pallas_call(main_kernel, grid=(steps,), in_specs=[pl.BlockSpec(up.shap...  13.2 us
    ppermute x4, starting transfers between devices, shifted(): return lax.ppermute(cells, axis, routes)  11.7 us
    pallas_call x1, Pallas kernels, base_logits(): pl.pallas_call(base_kernel, out_shape=[jax.ShapeDtypeStruct((count, 16, k...  5.35 us
    ppermute x4, waiting for transfers between devices, shifted(): return lax.ppermute(cells, axis, routes)  5.19 us
    unnamed x22, local copies, waits for them, and re-layouts  5.11 us
    pallas_call x1, Pallas kernels, turn(): pl.pallas_call(turn_kernel, grid=(row_count // step,), in_specs=[pl.Block...  4.08 us
    pallas_call x1, Pallas kernels, keys(): pl.pallas_call(keys_kernel, out_shape=[jax.ShapeDtypeStruct((2, count, 51...  3.99 us
  transfers between devices with their start and end apart: 6, of which 3 were waited for; matrix products, arithmetic and copies ran while one was open for 4% of the time, Pallas kernels for 22%

profile of v3, /device:TPU:4, one launch (start us, length us, event | category | flops | bytes accessed | tf_op | source)
XLA Modules:
  0.0 83.0 jit_solution(3249026034472033477)
XLA Ops:
  0.6 1.1 %fusion.1 = (bf16[64,8,256]{2,1,0:T(8,128)(2,1)S(1)}, bf16[64,8,256]{2,1,0:T(8,128)(2,1)S(1)}) fusion(bf16[64,64,256]{2,1,0:T(8,128)(2,1)} %pair_ref.1), kind=kLoop, calls=%fused_computation.2 | loop fusion | bytes 1048576 | tf_op jit(solution)/shard_map/slice | solution.py:682
  1.7 7.1 %collective-permute-start.1 = (bf16[64,8,256]{2,1,0:T(8,128)(2,1)S(1)}, bf16[64,8,256]{2,1,0:T(8,128)(2,1)S(1)}, u32[]{:S(2)}, u32[]{:S(2)}) collective-permute-start(bf16[64,8,256]{2,1,0:T(8,128)(2,1)S(1)} %get-tuple-element.48), channel_id=1, source_target_pairs={{8,0},{16,8},{24,16},{32,24},{40,32},{48,40},{56,48},{64,56},{72,6... | collective-permute-start | bytes 786440 | tf_op jit(solution)/shard_map/ppermute | solution.py:636
  8.9 1.9 %collective-permute-start = (bf16[64,8,256]{2,1,0:T(8,128)(2,1)S(1)}, bf16[64,8,256]{2,1,0:T(8,128)(2,1)S(1)}, u32[]{:S(2)}, u32[]{:S(2)}) collective-permute-start(bf16[64,8,256]{2,1,0:T(8,128)(2,1)S(1)} %get-tuple-element.49), channel_id=1, source_target_pairs={{0,8},{8,16},{16,24},{24,32},{32,40},{40,48},{48,56},{56,64},{64,7... | collective-permute-start | bytes 786440 | tf_op jit(solution)/shard_map/ppermute | solution.py:636
  10.8 1.9 %pack.1 = (bf16[88,384]{1,0:T(8,128)(2,1)}, f32[8,256]{1,0:T(8,128)}) custom-call(bf16[256,384]{1,0:T(8,128)(2,1)} %single_ref.3, f32[3,256]{1,0:T(4,128)} %quat_ref.1, f32[3,256]{1,0:T(4,128)} %trans_ref.1, s32[256]{0:T(256)} %chain_ref.1, s32[256]{0:T(256)} %mask_ref.1), custom_call_target="tpu_custom_call" | custom-call | tf_op jit(solution)/shard_map/pack/pallas_call | solution.py:594
  12.7 0.0 copy-start.8
  12.7 0.1 collective-permute-start.4
  12.8 4.1 %turn.1 = (bf16[64,64,256]{2,1,0:T(8,128)(2,1)}, bf16[8,64,64]{2,1,0:T(8,128)(2,1)}, bf16[8,64,64]{2,1,0:T(8,128)(2,1)}) custom-call(bf16[64,64,256]{2,1,0:T(8,128)(2,1)} %pair_ref.1), custom_call_target="tpu_custom_call" | custom-call | tf_op jit(solution)/shard_map/turn/pallas_call | solution.py:57
  16.9 4.0 %keys.1 = (bf16[2,256,512]{2,1,0:T(8,128)(2,1)}, bf16[3,256,384]{2,1,0:T(8,128)(2,1)}, f32[16,256]{1,0:T(8,128)}) custom-call(bf16[256,384]{1,0:T(8,128)(2,1)} %single_ref.3, bf16[192,384]{1,0:T(8,128)(2,1)} %bitcast.12, bf16[192,384]{1,0:T(8,128)(2,1)} %bitcast.13, bf16[432,384]{1,0:T(8,128)(2,1)} %bitcast.10, ...), custom_call_target="tpu_custom_call" | custom-call | tf_op jit(solution)/shard_map/keys/pallas_call | solution.py:406
  20.9 0.0 collective-permute-done.1.raw_down_ref
  20.9 3.7 %collective-permute-done.raw_up_ref = bf16[64,8,256]{2,1,0:T(8,128)(2,1)S(1)} collective-permute-done((bf16[64,8,256]{2,1,0:T(8,128)(2,1)S(1)}, bf16[64,8,256]{2,1,0:T(8,128)(2,1)S(1)}, u32[]{:S(2)}, u32[]{:S(2)}) %collective-permute-start) | collective-permute-done | bytes 262176 | tf_op jit(solution)/shard_map/ppermute | solution.py:636
  24.6 0.0 copy-done.2
  24.6 0.7 copy-done.3
  25.3 3.0 %rim.1 = (bf16[8,64,256]{2,1,0:T(8,128)(2,1)}, bf16[8,64,256]{2,1,0:T(8,128)(2,1)}, bf16[10,64,64]{2,1,0:T(8,128)(2,1)}, bf16[10,64,64]{2,1,0:T(8,128)(2,1)}) custom-call(bf16[64,8,256]{2,1,0:T(8,128)(2,1)} %copy-done.3, bf16[64,8,256]{2,1,0:T(8,128)(2,1)} %copy-done.2, bf16[8,64,64]{2,1,0:T(8,128)(2,1)} %get-tuple-element.28.own_head_ref, ...), custom_call_target="tpu_custom_call" | custom-call | tf_op jit(solution)/shard_map/rim/pallas_call | solution.py:111
  28.3 1.3 %collective-permute-start.2 = (bf16[10,64,64]{2,1,0:T(8,128)(2,1)}, bf16[10,64,64]{2,1,0:T(8,128)(2,1)S(1)}, u32[]{:S(2)}, u32[]{:S(2)}) collective-permute-start(bf16[10,64,64]{2,1,0:T(8,128)(2,1)} %get-tuple-element.35), channel_id=1, source_target_pairs={{0,1},{1,2},{2,3},{3,4},{4,5},{5,6},{6,7},{8,9},{9,10},{10,11},{11... | collective-permute-start | bytes 245768 | tf_op jit(solution)/shard_map/ppermute | solution.py:636
  29.6 1.3 %collective-permute-start.3 = (bf16[10,64,64]{2,1,0:T(8,128)(2,1)}, bf16[10,64,64]{2,1,0:T(8,128)(2,1)S(1)}, u32[]{:S(2)}, u32[]{:S(2)}) collective-permute-start(bf16[10,64,64]{2,1,0:T(8,128)(2,1)} %get-tuple-element.36), channel_id=1, source_target_pairs={{1,0},{2,1},{3,2},{4,3},{5,4},{6,5},{7,6},{9,8},{10,9},{11,10},{12... | collective-permute-start | bytes 245768 | tf_op jit(solution)/shard_map/ppermute | solution.py:636
  30.9 0.0 copy-done.9
  30.9 0.0 copy-done.6
  31.0 0.0 copy-done.7
  31.0 0.6 concatenate.3.params_ref
  31.7 0.0 collective-permute-done.4.query_ref.message_ref
  31.7 0.6 copy-done.1
  32.3 5.4 %base.1 = (f32[64,16,256]{2,1,0:T(8,128)}, f32[64,16]{1,0:T(8,128)}) custom-call(bf16[88,384]{1,0:T(8,128)(2,1)} %copy-done.1, bf16[192,384]{1,0:T(8,128)(2,1)} %bitcast.14, bf16[144,384]{1,0:T(8,128)(2,1)} %bitcast.15, bf16[3,256,384]{2,1,0:T(8,128)(2,1)} %get-tuple-element.38.key_ref, f32[16,256]{1,0:T(8,128)} %get-tuple-element.39.key_sq_ref, ...), custom_call_target="tpu_custom_call" | custom-call | tf_op jit(solution)/shard_map/base/pallas_call | solution.py:492
  37.7 0.0 collective-permute-done.2.left_ref
  37.7 1.5 %collective-permute-done.3.right_ref = bf16[10,64,64]{2,1,0:T(8,128)(2,1)S(1)} collective-permute-done((bf16[10,64,64]{2,1,0:T(8,128)(2,1)}, bf16[10,64,64]{2,1,0:T(8,128)(2,1)S(1)}, u32[]{:S(2)}, u32[]{:S(2)}) %collective-permute-start.3) | collective-permute-done | bytes 81952 | tf_op jit(solution)/shard_map/ppermute | solution.py:636
  39.1 0.6 copy-done.5
  39.8 13.2 %main.1 = (bf16[64,64,256]{2,1,0:T(8,128)(2,1)}, f32[64,16,128]{2,1,0:T(8,128)}) custom-call(bf16[8,64,256]{2,1,0:T(8,128)(2,1)} %get-tuple-element.30.up_ref, bf16[64,64,256]{2,1,0:T(8,128)(2,1)} %get-tuple-element.31.own_ref, bf16[8,64,256]{2,1,0:T(8,128)(2,1)} %get-tuple-element.32.down_ref, bf16[10,64,64]{2,1,0:T(8,128)(2,1)} %copy-done.4, ...), custom_call_target="tpu_custom_call" | custom-call | tf_op jit(solution)/shard_map/main/pallas_call | solution.py:307
  53.0 16.4 %all_to_all.10.sums_ref = f32[8,8,16,128]{3,2,1,0:T(8,128)} all-to-all(f32[8,8,16,128]{3,2,1,0:T(8,128)} %bitcast.9), channel_id=1, replica_groups=mesh['row'=32,'col'=8] {'col'}, dimensions={0} | all-to-all | bytes 1048576 | tf_op jit(solution)/shard_map/all_to_all | solution.py:739
  69.5 3.3 %finish.1 = bf16[8,8,384]{2,1,0:T(8,128)(2,1)} custom-call(f32[8,8,16,128]{3,2,1,0:T(8,128)} %all_to_all.10.sums_ref, f32[16,512]{1,0:T(8,128)} %constant.24.clone.owner_ref, f32[64,16]{1,0:T(8,128)} %get-tuple-element.45.frame_ref, bf16[88,384]{1,0:T(8,128)(2,1)} %copy-done.1, bf16[1248,384]{1,0:T(8,128)(2,1)} %w_out_ref.1, f32[8,384]{1,0:T(8,128)} %concatenate.3.params_ref), custom_call_target="tpu_custom_call" | custom-call | tf_op jit(solution)/shard_map/finish/pallas_call | solution.py:568
  72.8 3.3 %all-to-all-start.1 = ((bf16[8,8,384]{2,1,0:T(8,128)(2,1)}), bf16[8,8,384]{2,1,0:T(8,128)(2,1)S(1)}, u32[]{:S(2)}, u32[]{:S(2)}) async-start(bf16[8,8,384]{2,1,0:T(8,128)(2,1)} %finish.1), calls=%async_computation.1 | async-start | bytes 98304 | tf_op jit(solution)/shard_map/all_to_all | solution.py:741
  76.1 2.5 %copy.25 = bf16[64,64,256]{2,1,0:T(8,128)(2,1)} copy(bf16[64,64,256]{2,0,1:T(8,128)(2,1)S(1)} %bitcast.8) | data formatting | bytes 4194304
  78.6 3.7 %all-to-all-done.1 = bf16[8,8,384]{2,1,0:T(8,128)(2,1)S(1)} async-done(((bf16[8,8,384]{2,1,0:T(8,128)(2,1)}), bf16[8,8,384]{2,1,0:T(8,128)(2,1)S(1)}, u32[]{:S(2)}, u32[]{:S(2)}) %all-to-all-start.1) | async-done | bytes 49184 | tf_op jit(solution)/shard_map/all_to_all | solution.py:741
  82.3 0.6 copy.27
  (21 shorter events, 0.1 us)
Async XLA Ops:
  1.7 19.2 %collective-permute-start.1 = (bf16[64,8,256]{2,1,0:T(8,128)(2,1)S(1)}, bf16[64,8,256]{2,1,0:T(8,128)(2,1)S(1)}, u32[]{:S(2)}, u32[]{:S(2)}) collective-permute-start(bf16[64,8,256]{2,1,0:T(8,128)(2,1)S(1)} %get-tuple-element.48), channel_id=1, source_target_pairs={{8,0},{16,8},{24,16},{32,24},{40,32},{48,40},{56,48},{64,56},{72,6... | collective-permute-start | bytes 786440 | tf_op jit(solution)/shard_map/ppermute | solution.py:636
  8.9 15.7 %collective-permute-start = (bf16[64,8,256]{2,1,0:T(8,128)(2,1)S(1)}, bf16[64,8,256]{2,1,0:T(8,128)(2,1)S(1)}, u32[]{:S(2)}, u32[]{:S(2)}) collective-permute-start(bf16[64,8,256]{2,1,0:T(8,128)(2,1)S(1)} %get-tuple-element.49), channel_id=1, source_target_pairs={{0,8},{8,16},{16,24},{24,32},{32,40},{40,48},{48,56},{56,64},{64,7... | collective-permute-start | bytes 786440 | tf_op jit(solution)/shard_map/ppermute | solution.py:636
  12.7 18.2 %copy-start.9 = (f32[12]{0:T(128)S(1)}, f32[12]{0:T(128)}, u32[]{:S(2)}) copy-start(f32[12]{0:T(128)} %param.37) | copy-start | bytes 148
  12.7 18.3 %copy-start.6 = (f32[384]{0:T(512)S(1)}, f32[384]{0:T(512)}, u32[]{:S(2)}) copy-start(f32[384]{0:T(512)} %param.40) | copy-start | bytes 4612
  12.7 18.3 %copy-start.7 = (f32[64]{0:T(128)S(1)}, f32[64]{0:T(128)}, u32[]{:S(2)}) copy-start(f32[64]{0:T(128)} %param.25) | copy-start | bytes 772
  12.7 18.3 %copy-start.8 = (f32[12]{0:T(128)S(1)}, f32[12]{0:T(128)}, u32[]{:S(2)}) copy-start(f32[12]{0:T(128)} %param.38) | copy-start | bytes 148
  12.7 19.0 %collective-permute-start.4 = (bf16[88,384]{1,0:T(8,128)(2,1)}, bf16[88,384]{1,0:T(8,128)(2,1)S(1)}, u32[]{:S(2)}, u32[]{:S(2)}) collective-permute-start(bf16[88,384]{1,0:T(8,128)(2,1)} %get-tuple-element.37), channel_id=1, source_target_pairs={{0,2},{8,10},{16,18},{24,26},{32,3},{40,11},{48,19},{56,27},{64,0}... | collective-permute-start | bytes 202760 | tf_op jit(solution)/shard_map/ppermute | solution.py:685
  20.9 3.7 %copy-start.2 = (bf16[64,8,256]{2,1,0:T(8,128)(2,1)}, bf16[64,8,256]{2,1,0:T(8,128)(2,1)S(1)}, u32[]{:S(2)}) copy-start(bf16[64,8,256]{2,1,0:T(8,128)(2,1)S(1)} %collective-permute-done.1.raw_down_ref) | copy-start | bytes 786436
  24.6 0.7 copy-start.3
  28.3 9.4 %collective-permute-start.2 = (bf16[10,64,64]{2,1,0:T(8,128)(2,1)}, bf16[10,64,64]{2,1,0:T(8,128)(2,1)S(1)}, u32[]{:S(2)}, u32[]{:S(2)}) collective-permute-start(bf16[10,64,64]{2,1,0:T(8,128)(2,1)} %get-tuple-element.35), channel_id=1, source_target_pairs={{0,1},{1,2},{2,3},{3,4},{4,5},{5,6},{6,7},{8,9},{9,10},{10,11},{11... | collective-permute-start | bytes 245768 | tf_op jit(solution)/shard_map/ppermute | solution.py:636
  29.6 9.5 %collective-permute-start.3 = (bf16[10,64,64]{2,1,0:T(8,128)(2,1)}, bf16[10,64,64]{2,1,0:T(8,128)(2,1)S(1)}, u32[]{:S(2)}, u32[]{:S(2)}) collective-permute-start(bf16[10,64,64]{2,1,0:T(8,128)(2,1)} %get-tuple-element.36), channel_id=1, source_target_pairs={{1,0},{2,1},{3,2},{4,3},{5,4},{6,5},{7,6},{9,8},{10,9},{11,10},{12... | collective-permute-start | bytes 245768 | tf_op jit(solution)/shard_map/ppermute | solution.py:636
  31.7 0.6 copy-start.1
  37.7 1.5 %copy-start.4 = (bf16[10,64,64]{2,1,0:T(8,128)(2,1)}, bf16[10,64,64]{2,1,0:T(8,128)(2,1)S(1)}, u32[]{:S(2)}) copy-start(bf16[10,64,64]{2,1,0:T(8,128)(2,1)S(1)} %collective-permute-done.2.left_ref) | copy-start | bytes 245764
  39.1 0.7 copy-start.5
  53.0 23.1 %copy-start = (bf16[64,64,256]{2,1,0:T(8,128)(2,1)S(1)}, bf16[64,64,256]{2,1,0:T(8,128)(2,1)}, u32[]{:S(2)}) copy-start(bf16[64,64,256]{2,1,0:T(8,128)(2,1)} %get-tuple-element.43) | copy-start | bytes 6291460
  72.8 9.6 %all-to-all-start.1 = ((bf16[8,8,384]{2,1,0:T(8,128)(2,1)}), bf16[8,8,384]{2,1,0:T(8,128)(2,1)S(1)}, u32[]{:S(2)}, u32[]{:S(2)}) async-start(bf16[8,8,384]{2,1,0:T(8,128)(2,1)} %finish.1), calls=%async_computation.1 | async-start | bytes 98304 | tf_op jit(solution)/shard_map/all_to_all | solution.py:741
